TPU v7x, 256 devices: a whole 4x4x8 slice. The times are simulated.
256 devices in a mesh: side: 2 (over core), grp: 4 (over y), blk: 32 (over x, z).
Axes of the slice: x: 4, y: 4, z: 8, core: 2. Of those that a mesh axis runs over, the one named last changes fastest.
Arguments:
- node_modes: bfloat16 [3, 131072, 256], P(None, ('grp', 'blk'), 'side'), may hold values from -6 to 6
- node_index: int32 [4, 196608], P(None, ('grp', 'blk')), may hold values from 0 to 1023
- interp: float32 [4, 196608], P(None, ('grp', 'blk')), may hold values from 0.1 to 1
- normals: float32 [3, 196608], P(None, ('grp', 'blk')), may hold values from -6 to 6
- counts: int32 [128, 128], P(None, ('grp', 'blk')), may hold values from 0 to 12, as said below
- inverse_diag: bfloat16 [131072, 1024], P(('grp', 'blk'))
- lower_left: bfloat16 [131072, 32], P(('grp', 'blk')), may hold values from -0.375 to 0.375
- lower_right: bfloat16 [131072, 32], P(('grp', 'blk')), may hold values from -0.03125 to 0.03125
- upper_left: bfloat16 [131072, 32], P(('grp', 'blk')), may hold values from -0.375 to 0.375
- upper_right: bfloat16 [131072, 32], P(('grp', 'blk')), may hold values from -0.03125 to 0.03125
- ranks: int32 [128], P(('grp', 'blk')), may hold values from 8 to 32
- areas: float32 [131072], P(('grp', 'blk')), may hold values from 0.0013810679 to 0.011048543
Outputs:
- potentials: bfloat16 [131072, 256], P(('grp', 'blk'), 'side')
- added_mass: float32 [256, 256], P(('grp', 'blk'), 'side')
Inputs may be any that keep to these rules, and one draw needn't show every extreme that they name: In each column d the counts sum to 1024, and every column holds one count equal to 12.
All inputs are finite; a program needn't handle non-finite values.
Results may differ from a plain program's by a relative error of at most 0.0049.
Values may be sent and summed in bfloat16 or wider, within the bound.
No kernel may reach another device: no remote copies, remote signals or barrier semaphores. Data moves between devices by JAX's collectives and lax.ppermute only.
A program may use at most 64 MiB of HBM per device.

v0:
```python
import functools
import jax
import jax.numpy as jnp
from jax import lax
from jax.experimental import pallas as pl
from jax.experimental.pallas import tpu as pltpu
from jax.sharding import PartitionSpec as P

F32, BF16, I32 = jnp.float32, jnp.bfloat16, jnp.int32
AXES = ("y", "x", "z")
RANK, CAP, SLOT_ROWS, WIDE = 32, 12, 16, 256
PARAMS = pltpu.CompilerParams(vmem_limit_bytes=28 * 1024 * 1024)
VMEM = pl.BlockSpec(memory_space=pltpu.VMEM)
SMEM = pl.BlockSpec(memory_space=pltpu.SMEM)


def mm(a, b):
    return lax.dot_general(a, b, (((1,), (0,)), ((), ())), preferred_element_type=F32)


def mm_t(a, b):
    return lax.dot_general(a, b, (((1,), (1,)), ((), ())), preferred_element_type=F32)


def halves(value):
    high = value.astype(BF16)
    return high, (value - high.astype(F32)).astype(BF16)


def tall(value):
    high, low = halves(value)
    return jnp.concatenate([high, high, low], axis=0)


def interp_kernel(modes_ref, index_ref, interp_ref, normals_ref, out_ref):
    chunk = index_ref.shape[1]
    nodes = modes_ref.shape[1]
    rows = jnp.concatenate(
        [
            index_ref[...].astype(F32),
            interp_ref[...],
            normals_ref[...],
            jnp.zeros((5, chunk), F32),
        ],
        axis=0,
    )
    columns = rows.T
    node = lax.broadcasted_iota(I32, (chunk, nodes), 1).astype(F32)
    mix = jnp.zeros((chunk, nodes), F32)
    for corner in range(4):
        here = columns[:, corner : corner + 1] == node
        mix = mix + jnp.where(here, columns[:, 4 + corner : 5 + corner], 0.0)
    table = jnp.concatenate([modes_ref[0], modes_ref[1], modes_ref[2]], axis=1)
    high, low = halves(mix)
    picked = mm(high, table) + mm(low, table)
    width = modes_ref.shape[2]
    velocity = jnp.zeros((chunk, width), F32)
    for axis_id in range(3):
        part = picked[:, axis_id * width : (axis_id + 1) * width]
        velocity = velocity + columns[:, 8 + axis_id : 9 + axis_id] * part
    pairs = velocity.reshape(chunk // 24, 24, width)
    out_ref[:, 0:16, :] = pairs[:, 0:16, :].astype(BF16)
    out_ref[:, 16:32, :] = pairs[:, 8:24, :].astype(BF16)


def interpolate(node_modes, node_index, interp, normals):
    slots, width = node_index.shape[1], node_modes.shape[2]
    steps = 4
    chunk = slots // steps
    return pl.pallas_call(
        interp_kernel,
        grid=(steps,),
        in_specs=[
            pl.BlockSpec(node_modes.shape, lambda i: (0, 0, 0)),
            pl.BlockSpec((4, chunk), lambda i: (0, i)),
            pl.BlockSpec((4, chunk), lambda i: (0, i)),
            pl.BlockSpec((3, chunk), lambda i: (0, i)),
        ],
        out_specs=pl.BlockSpec((chunk // 24, 32, width), lambda i: (i, 0, 0)),
        out_shape=jax.ShapeDtypeStruct((slots // 24, 32, width), BF16),
        compiler_params=PARAMS,
        cost_estimate=pl.CostEstimate(
            flops=2 * slots * 1024 * 384, bytes_accessed=1 << 20, transcendentals=0
        ),
    )(node_modes, node_index, interp, normals)


def prepare_kernel(
    place_ref, rank_ref, count_ref, diag_ref, lower_ref, right_ref, upper_ref, back_ref,
    stack_ref, mats_ref, target_ref,
):
    panels = diag_ref.shape[0]
    keep = lax.broadcasted_iota(I32, (RANK, panels), 0) < rank_ref[0]
    zero = jnp.zeros((RANK, panels), BF16)
    lower = jnp.where(keep, lower_ref[...], zero)
    upper = jnp.where(keep, upper_ref[...], zero)
    spread = mm_t(diag_ref[...], lower)
    high, low = halves(spread)
    both = jnp.concatenate([right_ref[...], back_ref[...]], axis=0)
    seen = mm(both, jnp.concatenate([high, low], axis=1))
    seen = seen[:, :RANK] + seen[:, RANK:]
    back = mm_t(back_ref[...], upper)
    blank = jnp.zeros((RANK, RANK), F32)
    mats = jnp.concatenate([-seen[:RANK], -back, seen[RANK:], blank], axis=1)
    mats_high, mats_low = halves(mats)
    mats_ref[...] = jnp.concatenate([mats_high, mats_low], axis=0)
    stack_ref[...] = jnp.concatenate(
        [high, upper.astype(F32).T.astype(BF16), low, jnp.zeros((panels, RANK), BF16)], axis=1
    )
    sources = count_ref.shape[1]
    slots = target_ref.shape[1]
    counts = jnp.broadcast_to(count_ref[...].astype(F32), (16, sources)).astype(BF16)
    source = lax.broadcasted_iota(I32, (sources, slots), 0)
    column = lax.broadcasted_iota(I32, (sources, slots), 1) // SLOT_ROWS
    start = mm(counts, jnp.where(source < column, 1.0, 0.0).astype(BF16))[0:1]
    mine = mm(counts, jnp.where(source == column, 1.0, 0.0).astype(BF16))[0:1]
    slot = lax.broadcasted_iota(I32, (1, slots), 1) % SLOT_ROWS - 4 * place_ref[3]
    slot = slot.astype(F32)
    target_ref[...] = jnp.where((slot >= 0.0) & (slot < mine), start + slot, -1.0)


def prepare(place, rank, count, diag, lower, right, upper, back):
    panels, slots = diag.shape[0], count.shape[1] * SLOT_ROWS
    return pl.pallas_call(
        prepare_kernel,
        in_specs=[SMEM, SMEM] + [VMEM] * 6,
        out_specs=[VMEM] * 3,
        out_shape=[
            jax.ShapeDtypeStruct((panels, 4 * RANK), BF16),
            jax.ShapeDtypeStruct((2 * RANK, 4 * RANK), BF16),
            jax.ShapeDtypeStruct((1, slots), F32),
        ],
        compiler_params=PARAMS,
        cost_estimate=pl.CostEstimate(
            flops=4 << 30, bytes_accessed=8 << 20, transcendentals=0
        ),
    )(place, rank, count, diag, lower, right, upper, back)


def solve_kernel(
    arrived_ref, target_ref, diag_ref, right_ref, back_ref, mats_ref,
    solved_ref, turned_ref, send_ref,
):
    panels = diag_ref.shape[0]
    slots = target_ref.shape[1]
    step = 256
    target = target_ref[...]
    arrived = arrived_ref[...]
    parts = []
    for begin in range(0, panels, step):
        panel = (lax.broadcasted_iota(I32, (step, slots), 0) + begin).astype(F32)
        pick = jnp.where(panel == target, 1.0, 0.0).astype(BF16)
        parts.append(mm(pick, arrived))
    normal = jnp.concatenate(parts, axis=0)
    turned_ref[...] = normal.T.astype(BF16)
    solved = mm(diag_ref[...], normal.astype(BF16))
    solved_ref[...] = solved
    high, low = halves(solved)
    width = solved.shape[1]
    both = jnp.concatenate([right_ref[...], back_ref[...]], axis=0)
    seen = mm(both, jnp.concatenate([high, low], axis=1))
    seen = (seen[:, :width] + seen[:, width:]).astype(BF16)
    message = jnp.concatenate([seen, mats_ref[...]], axis=0)
    send_ref[...] = jnp.broadcast_to(message[None], send_ref.shape)


def solve(arrived, target, diag, right, back, mats, peers):
    panels, width = diag.shape[0], arrived.shape[1]
    return pl.pallas_call(
        solve_kernel,
        in_specs=[VMEM] * 6,
        out_specs=[VMEM] * 3,
        out_shape=[
            jax.ShapeDtypeStruct((panels, width), F32),
            jax.ShapeDtypeStruct((width, panels), BF16),
            jax.ShapeDtypeStruct((peers, 4 * RANK, width), BF16),
        ],
        compiler_params=PARAMS,
        cost_estimate=pl.CostEstimate(
            flops=1 << 30, bytes_accessed=4 << 20, transcendentals=0
        ),
    )(arrived, target, diag, right, back, mats)


def element(ref, position):
    high = ref[position, 2 * RANK : 3 * RANK, :]
    low = ref[position, 3 * RANK : 4 * RANK, :]

    def wide(which):
        lanes = slice(which * RANK, (which + 1) * RANK)
        return jnp.concatenate([high[:, lanes], low[:, lanes], high[:, lanes]], axis=1)

    vectors = ref[position, 0 : 2 * RANK, :].astype(F32)
    ahead = jnp.concatenate([wide(0), wide(2)], axis=0)
    return vectors[:RANK], vectors[RANK:], ahead, wide(1)


def chain(ref, mine, first, last, lift):
    count = ref.shape[0]
    elements = [element(ref, position) for position in range(count)]
    forward, own_forward, given = first, jnp.zeros_like(first), []
    for position in range(count):
        shift, gain, ahead, _ = elements[position]
        own_forward = jnp.where(mine == position, forward, own_forward)
        moved = mm(ahead, tall(forward))
        given.append(lift(gain) - moved[RANK:])
        forward = forward + moved[:RANK] + lift(shift)
    backward, own_backward = last, jnp.zeros_like(last)
    for position in reversed(range(count)):
        own_backward = jnp.where(mine == position, backward, own_backward)
        backward = backward + mm(elements[position][3], tall(backward)) + given[position]
    return forward, backward, own_forward, own_backward


def unit(offset):
    row = lax.broadcasted_iota(I32, (RANK, WIDE), 0)
    lane = lax.broadcasted_iota(I32, (RANK, WIDE), 1)
    return jnp.where(lane == row + offset, 1.0, 0.0).astype(F32)


def inner_kernel(place_ref, got_ref, own_ref, send_ref):
    width = got_ref.shape[2]
    pad = jnp.zeros((RANK, WIDE - width), F32)
    lift = lambda value: jnp.concatenate([value, pad], axis=1)
    in_t, in_s = width, width + RANK
    forward, backward, own_s, own_t = chain(
        got_ref, place_ref[0], unit(in_s), unit(in_t), lift
    )
    own_ref[...] = jnp.concatenate([own_s, own_t], axis=0)
    eye = unit(0)[:, :RANK]
    mats = jnp.concatenate(
        [
            forward[:, in_s : in_s + RANK] - eye,
            backward[:, in_t : in_t + RANK] - eye,
            -backward[:, in_s : in_s + RANK],
            jnp.zeros((RANK, RANK), F32),
        ],
        axis=1,
    )
    high, low = halves(mats)
    message = jnp.concatenate(
        [forward[:, :width].astype(BF16), backward[:, :width].astype(BF16), high, low], axis=0
    )
    send_ref[...] = jnp.broadcast_to(message[None], send_ref.shape)


def inner(place, got, peers):
    return pl.pallas_call(
        inner_kernel,
        in_specs=[SMEM, VMEM],
        out_specs=[VMEM] * 2,
        out_shape=[
            jax.ShapeDtypeStruct((2 * RANK, WIDE), F32),
            jax.ShapeDtypeStruct((peers,) + got.shape[1:], BF16),
        ],
        compiler_params=PARAMS,
    )(place, got)


def outer_kernel(
    place_ref, got_ref, own_ref, solved_ref, stack_ref, turned_ref, other_ref, area_ref,
    potential_ref, mass_ref,
):
    width = got_ref.shape[2]
    panels = solved_ref.shape[0]
    zero = jnp.zeros((RANK, width), F32)
    _, _, in_s, in_t = chain(got_ref, place_ref[1], zero, zero, lambda value: value)
    own = own_ref[...]
    map_high, map_low = halves(own[:, width : width + 2 * RANK])
    maps = jnp.concatenate([map_high, map_low, map_high], axis=1)
    state = own[:, :width] + mm(maps, tall(jnp.concatenate([in_t, in_s], axis=0)))
    high, low = halves(state)
    blank = jnp.zeros((RANK, width), BF16)
    left = jnp.concatenate([high, high[:RANK], blank], axis=0)
    right = jnp.concatenate([low, blank, blank], axis=0)
    fixed = mm(stack_ref[...], jnp.concatenate([left, right], axis=1))
    potential = (solved_ref[...] - (fixed[:, :width] + fixed[:, width:])).astype(BF16)
    potential_ref[...] = potential
    area = jnp.broadcast_to(area_ref[...], (8, panels)).T[:, 0:1]
    weighted = (area * potential.astype(F32)).astype(BF16)
    side = place_ref[2]
    mass_ref[pl.ds(pl.multiple_of(side * width, width), width), :] = mm(turned_ref[...], weighted)
    mass_ref[pl.ds(pl.multiple_of((1 - side) * width, width), width), :] = mm(
        other_ref[...], weighted
    )


def outer(place, got, own, solved, stack, turned, other, area):
    panels, width = solved.shape
    return pl.pallas_call(
        outer_kernel,
        in_specs=[SMEM] + [VMEM] * 7,
        out_specs=[VMEM] * 2,
        out_shape=[
            jax.ShapeDtypeStruct((panels, width), BF16),
            jax.ShapeDtypeStruct((2 * width, width), F32),
        ],
        compiler_params=PARAMS,
    )(place, got, own, solved, stack, turned, other, area)


def body(
    node_modes, node_index, interp, normals, counts, inverse_diag,
    lower_left, lower_right, upper_left, upper_right, ranks, areas,
):
    devices, width = lax.axis_size(AXES), node_modes.shape[2]
    inner_size, outer_size = lax.axis_size("z"), lax.axis_size(("y", "x"))
    depth, group = lax.axis_index("z"), lax.axis_index(("y", "x"))
    place = jnp.stack([depth, group, lax.axis_index("side"), depth % 2]).astype(I32)
    outgoing = interpolate(node_modes, node_index, interp, normals)
    arrived = lax.all_to_all(
        outgoing.reshape(devices, SLOT_ROWS, width), AXES, split_axis=0, concat_axis=0, tiled=True
    ).reshape(devices * SLOT_ROWS, width)
    right, back = lower_right.T, upper_right.T
    stack, mats, target = prepare(
        place, ranks, counts.reshape(1, devices), inverse_diag, lower_left.T, right,
        upper_left.T, back,
    )
    solved, turned, send = solve(
        arrived, target, inverse_diag, right, back, mats, inner_size
    )
    other = lax.ppermute(turned, "side", [(0, 1), (1, 0)])
    got = lax.all_to_all(send, "z", split_axis=0, concat_axis=0, tiled=True)
    own, send = inner(place, got, outer_size)
    got = lax.all_to_all(send, ("y", "x"), split_axis=0, concat_axis=0, tiled=True)
    potentials, mass = outer(
        place, got, own, solved, stack, turned, other, areas.reshape(1, -1)
    )
    rows = mass.shape[0] // devices
    pieces = lax.all_to_all(
        mass.reshape(devices, rows, width), AXES, split_axis=0, concat_axis=0, tiled=True
    )
    return potentials, jnp.sum(pieces, axis=0)


def solution(mesh):
    grid = jax.sharding.Mesh(mesh.devices.reshape(2, 4, 4, 8), ("side",) + AXES)
    in_specs = (
        P(None, AXES, "side"),
        P(None, AXES),
        P(None, AXES),
        P(None, AXES),
        P(None, AXES),
        P(AXES, None),
        P(AXES, None),
        P(AXES, None),
        P(AXES, None),
        P(AXES, None),
        P(AXES),
        P(AXES),
    )
    out_specs = (P(AXES, "side"), P(AXES, "side"))
    return jax.shard_map(body, mesh=grid, in_specs=in_specs, out_specs=out_specs, check_vma=False)
```

profile of v0, /device:TPU:2, one launch (start us, length us, event | category | flops | bytes accessed | tf_op | source)
XLA Modules:
  0.0 105.2 jit_solution(9654518847560839194)
XLA Ops:
  0.6 0.0 copy-start.3
  0.6 1.1 %copy-done.3 = bf16[3,1024,128]{2,1,0:T(8,128)(2,1)S(1)} copy-done((bf16[3,1024,128]{2,1,0:T(8,128)(2,1)S(1)}, bf16[3,1024,128]{2,1,0:T(8,128)(2,1)}, u32[]{:S(2)}) %copy-start.3) | copy-done | bytes 786456
  1.8 0.0 copy-start.8
  1.8 0.7 copy-done.8
  2.5 0.0 copy-start.9
  2.5 0.7 copy-done.9
  3.2 0.7 copy-done.10
  4.0 0.0 copy-start.11
  4.0 7.7 %shard_map.131 = bf16[64,32,128]{2,1,0:T(8,128)(2,1)} custom-call(bf16[3,1024,128]{2,1,0:T(8,128)(2,1)S(1)} %copy-done.3, s32[4,1536]{1,0:T(4,128)S(1)} %copy-done.8, f32[4,1536]{1,0:T(4,128)S(1)} %copy-done.9, f32[3,1536]{1,0:T(4,128)S(1)} %copy-done.10), custom_call_target="tpu_custom_call" | custom-call | flops 1207959552 | bytes 1048576 | tf_op jit(solution)/shard_map/pallas_call | solution.py:70
  11.7 15.4 %all-to-all-start = ((bf16[128,16,128]{2,1,0:T(8,128)(2,1)}), bf16[128,16,128]{2,1,0:T(8,128)(2,1)S(1)}, u32[]{:S(2)}, u32[]{:S(2)}) async-start(bf16[128,16,128]{2,1,0:T(8,128)(2,1)} %bitcast.4), calls=%async_computation | async-start | bytes 1048576 | tf_op jit(solution)/shard_map/all_to_all | solution.py:311
  27.8 0.1 pad_add_fusion.place_ref
  27.9 0.0 copy-done.4
  27.9 0.0 copy-done.5
  27.9 0.0 copy-done.6
  27.9 0.0 copy-done.7
  27.9 0.0 copy-done.11
  27.9 0.0 copy-start.1
  27.9 1.6 %copy-done.1 = bf16[1024,1024]{1,0:T(8,128)(2,1)S(1)} copy-done((bf16[1024,1024]{1,0:T(8,128)(2,1)S(1)}, bf16[1024,1024]{1,0:T(8,128)(2,1)}, u32[]{:S(2)}) %copy-start.1) | copy-done | bytes 2097176
  29.5 1.8 %shard_map.132 = (bf16[1024,128]{1,0:T(8,128)(2,1)S(1)}, bf16[64,128]{1,0:T(8,128)(2,1)S(1)}, f32[1,2048]{1,0:T(1,128)S(1)}) custom-call(s32[4]{0:T(128)S(1)} %pad_add_fusion.place_ref, s32[1]{0:T(128)S(6)} %copy.14.rank_ref, s32[1,128]{1,0:T(1,128)S(1)} %bitcast.22, bf16[1024,1024]{1,0:T(8,128)(2,1)S(1)} %copy-done.1, bf16[32,1024]{1,0:T(8,128)(2,1)S(1)} %bitcast.16, ...), custom_call_target="tpu_custom_call" | custom-call | flops 4294967296 | bytes 8388608 | tf_op jit(solution)/shard_map/pallas_call | solution.py:124
  31.3 14.2 %all-to-all-done = bf16[128,16,128]{2,1,0:T(8,128)(2,1)S(1)} async-done(((bf16[128,16,128]{2,1,0:T(8,128)(2,1)}), bf16[128,16,128]{2,1,0:T(8,128)(2,1)S(1)}, u32[]{:S(2)}, u32[]{:S(2)}) %all-to-all-start) | async-done | bytes 524320 | tf_op jit(solution)/shard_map/all_to_all | solution.py:311
  45.5 1.6 %copy-done.2 = bf16[1024,1024]{1,0:T(8,128)(2,1)S(1)} copy-done((bf16[1024,1024]{1,0:T(8,128)(2,1)S(1)}, bf16[1024,1024]{1,0:T(8,128)(2,1)}, u32[]{:S(2)}) %copy-start.2) | copy-done | bytes 2097176
  47.1 2.0 %shard_map.133 = (f32[1024,128]{1,0:T(8,128)S(1)}, bf16[128,1024]{1,0:T(8,128)(2,1)S(1)}, bf16[8,128,128]{2,1,0:T(8,128)(2,1)S(1)}) custom-call(bf16[2048,128]{1,0:T(8,128)(2,1)S(1)} %bitcast.13, f32[1,2048]{1,0:T(1,128)S(1)} %get-tuple-element.12.target_ref, bf16[1024,1024]{1,0:T(8,128)(2,1)S(1)} %copy-done.2, bf16[32,1024]{1,0:T(8,128)(2,1)S(1)} %bitcast.19, ...), custom_call_target="tpu_custom_call" | custom-call | flops 1073741824 | bytes 4194304 | tf_op jit(solution)/shard_map/pallas_call | solution.py:169
  49.1 13.6 %all_to_all.20.got_ref = bf16[8,128,128]{2,1,0:T(8,128)(2,1)S(1)} all-to-all(bf16[8,128,128]{2,1,0:T(8,128)(2,1)S(1)} %get-tuple-element.14), channel_id=1, replica_groups=mesh['side'=2,'y'=4,'x'=4,'z'=8] {'z'}, dimensions={0} | all-to-all | bytes 524288 | tf_op jit(solution)/shard_map/all_to_all | solution.py:323
  62.7 3.5 %shard_map.134 = (f32[64,256]{1,0:T(8,128)S(1)}, bf16[16,128,128]{2,1,0:T(8,128)(2,1)}) custom-call(s32[4]{0:T(128)S(1)} %pad_add_fusion.place_ref, bf16[8,128,128]{2,1,0:T(8,128)(2,1)S(1)} %all_to_all.20.got_ref), custom_call_target="tpu_custom_call" | custom-call | tf_op jit(solution)/shard_map/pallas_call | solution.py:248
  66.2 5.9 %all-to-all-start.2 = ((bf16[16,128,128]{2,1,0:T(8,128)(2,1)}), bf16[16,128,128]{2,1,0:T(8,128)(2,1)S(1)}, u32[]{:S(2)}, u32[]{:S(2)}) async-start(bf16[16,128,128]{2,1,0:T(8,128)(2,1)} %get-tuple-element.15), calls=%async_computation.2 | async-start | bytes 1048576 | tf_op jit(solution)/shard_map/all_to_all | solution.py:325
  72.1 0.0 collective-permute-start
  72.2 1.5 %collective-permute-done.other_ref = bf16[128,1024]{1,0:T(8,128)(2,1)S(1)} collective-permute-done((bf16[128,1024]{1,0:T(8,128)(2,1)S(1)}, bf16[128,1024]{1,0:T(8,128)(2,1)S(1)}, u32[]{:S(2)}, u32[]{:S(2)}) %collective-permute-start) | collective-permute-done | bytes 262176 | tf_op jit(solution)/shard_map/ppermute | solution.py:322
  73.7 7.3 %all-to-all-done.2.got_ref = bf16[16,128,128]{2,1,0:T(8,128)(2,1)S(1)} async-done(((bf16[16,128,128]{2,1,0:T(8,128)(2,1)}), bf16[16,128,128]{2,1,0:T(8,128)(2,1)S(1)}, u32[]{:S(2)}, u32[]{:S(2)}) %all-to-all-start.2) | async-done | bytes 524320 | tf_op jit(solution)/shard_map/all_to_all | solution.py:325
  81.0 0.0 copy-done
  81.0 6.0 %shard_map.135 = (bf16[1024,128]{1,0:T(8,128)(2,1)}, f32[256,128]{1,0:T(8,128)S(1)}) custom-call(s32[4]{0:T(128)S(1)} %pad_add_fusion.place_ref, bf16[16,128,128]{2,1,0:T(8,128)(2,1)S(1)} %all-to-all-done.2.got_ref, f32[64,256]{1,0:T(8,128)S(1)} %get-tuple-element.16.own_ref, f32[1024,128]{1,0:T(8,128)S(1)} %get-tuple-element.17.solved_ref, ...), custom_call_target="tpu_custom_call" | custom-call | tf_op jit(solution)/shard_map/pallas_call | solution.py:290
  87.0 17.5 %all_to_all.21 = f32[128,2,128]{2,1,0:T(2,128)S(1)} all-to-all(f32[128,2,128]{2,1,0:T(2,128)S(1)} %bitcast.14), channel_id=1, replica_groups=mesh['side'=2,'y'=4,'x'=4,'z'=8] {'y','x','z'}, dimensions={0} | all-to-all | bytes 262144 | tf_op jit(solution)/shard_map/all_to_all | solution.py:330
  104.5 0.7 reduce_sum.9
  (7 shorter events, 0.0 us)
Async XLA Ops:
  0.6 1.1 %copy-start.3 = (bf16[3,1024,128]{2,1,0:T(8,128)(2,1)S(1)}, bf16[3,1024,128]{2,1,0:T(8,128)(2,1)}, u32[]{:S(2)}) copy-start(bf16[3,1024,128]{2,1,0:T(8,128)(2,1)} %modes_ref.1) | copy-start | bytes 2359300
  1.8 0.7 copy-start.8
  2.5 0.7 copy-start.9
  3.2 0.7 copy-start.10
  4.0 23.9 %copy-start.4 = (bf16[1024,32]{0,1:T(8,128)(2,1)S(1)}, bf16[1024,32]{0,1:T(8,128)(2,1)}, u32[]{:S(2)}) copy-start(bf16[1024,32]{0,1:T(8,128)(2,1)} %param.18) | copy-start | bytes 196612
  4.0 23.9 %copy-start.5 = (bf16[1024,32]{0,1:T(8,128)(2,1)S(1)}, bf16[1024,32]{0,1:T(8,128)(2,1)}, u32[]{:S(2)}) copy-start(bf16[1024,32]{0,1:T(8,128)(2,1)} %param.20) | copy-start | bytes 196612
  4.0 23.9 %copy-start.6 = (bf16[1024,32]{0,1:T(8,128)(2,1)S(1)}, bf16[1024,32]{0,1:T(8,128)(2,1)}, u32[]{:S(2)}) copy-start(bf16[1024,32]{0,1:T(8,128)(2,1)} %param.19) | copy-start | bytes 196612
  4.0 23.9 %copy-start.7 = (bf16[1024,32]{0,1:T(8,128)(2,1)S(1)}, bf16[1024,32]{0,1:T(8,128)(2,1)}, u32[]{:S(2)}) copy-start(bf16[1024,32]{0,1:T(8,128)(2,1)} %param.21) | copy-start | bytes 196612
  4.0 23.9 %copy-start.11 = (s32[128,1]{0,1:T(1,128)S(1)}, s32[128,1]{0,1:T(1,128)}, u32[]{:S(2)}) copy-start(s32[128,1]{0,1:T(1,128)} %param.16) | copy-start | bytes 1540
  11.7 33.8 %all-to-all-start = ((bf16[128,16,128]{2,1,0:T(8,128)(2,1)}), bf16[128,16,128]{2,1,0:T(8,128)(2,1)S(1)}, u32[]{:S(2)}, u32[]{:S(2)}) async-start(bf16[128,16,128]{2,1,0:T(8,128)(2,1)} %bitcast.4), calls=%async_computation | async-start | bytes 1048576 | tf_op jit(solution)/shard_map/all_to_all | solution.py:311
  27.9 1.6 %copy-start.1 = (bf16[1024,1024]{1,0:T(8,128)(2,1)S(1)}, bf16[1024,1024]{1,0:T(8,128)(2,1)}, u32[]{:S(2)}) copy-start(bf16[1024,1024]{1,0:T(8,128)(2,1)} %diag_ref.3) | copy-start | bytes 6291460
  45.5 1.6 %copy-start.2 = (bf16[1024,1024]{1,0:T(8,128)(2,1)S(1)}, bf16[1024,1024]{1,0:T(8,128)(2,1)}, u32[]{:S(2)}) copy-start(bf16[1024,1024]{1,0:T(8,128)(2,1)} %diag_ref.3) | copy-start | bytes 6291460
  47.1 33.9 %copy-start = (f32[1024]{0:T(1024)S(1)}, f32[1024]{0:T(1024)}, u32[]{:S(2)}) copy-start(f32[1024]{0:T(1024)} %param.23) | copy-start | bytes 12292
  66.2 14.8 %all-to-all-start.2 = ((bf16[16,128,128]{2,1,0:T(8,128)(2,1)}), bf16[16,128,128]{2,1,0:T(8,128)(2,1)S(1)}, u32[]{:S(2)}, u32[]{:S(2)}) async-start(bf16[16,128,128]{2,1,0:T(8,128)(2,1)} %get-tuple-element.15), calls=%async_computation.2 | async-start | bytes 1048576 | tf_op jit(solution)/shard_map/all_to_all | solution.py:325
  72.1 1.5 %collective-permute-start = (bf16[128,1024]{1,0:T(8,128)(2,1)S(1)}, bf16[128,1024]{1,0:T(8,128)(2,1)S(1)}, u32[]{:S(2)}, u32[]{:S(2)}) collective-permute-start(bf16[128,1024]{1,0:T(8,128)(2,1)S(1)} %get-tuple-element.19.turned_ref), channel_id=1, source_target_pairs={{0,128},{128,0},{1,129},{129,1},{2,130},{130,2},{3,131},{131,3},{4... | collective-permute-start | bytes 786440 | tf_op jit(solution)/shard_map/ppermute | solution.py:322
where the time goes:
time: 106 us; the launch traced here: 105 us
  blocking collectives  31.1 us (29%)
  waiting for transfers between devices  23 us (22%)
  starting transfers between devices  21.4 us (20%)
  Pallas kernels  21 us (20%)
  local copies, waits for them, and re-layouts  6.54 us (6%)
  between operations  1.38 us (1%)
    all_to_all x1, blocking collectives, body(): lax.all_to_all(mass.reshape(devices, rows, width), AXES, split_axis=0, co...  17.5 us
    all_to_all x1, starting transfers between devices, body(): lax.all_to_all(outgoing.reshape(devices, SLOT_ROWS, width), AXES, split_a...  15.4 us
    all_to_all x1, waiting for transfers between devices, body(): lax.all_to_all(outgoing.reshape(devices, SLOT_ROWS, width), AXES, split_a...  14.2 us
    all_to_all x1, blocking collectives, body(): got = lax.all_to_all(send, 'z', split_axis=0, concat_axis=0, tiled=True)  13.6 us
    pallas_call x1, Pallas kernels, interpolate(): pl.pallas_call(interp_kernel, grid=(steps,), in_specs=[pl.BlockSpec(node_...  7.72 us
    all_to_all x1, waiting for transfers between devices, body(): lax.all_to_all(send, ('y', 'x'), split_axis=0, concat_axis=0, tiled=True)  7.33 us
    unnamed x24, local copies, waits for them, and re-layouts  6.54 us
    pallas_call x1, Pallas kernels, outer(): pl.pallas_call(outer_kernel, in_specs=[SMEM] + [VMEM] * 7, out_specs=[VME...  5.97 us
  transfers between devices with their start and end apart: 3, of which 3 were waited for; matrix products, arithmetic and copies ran while one was open for 0% of the time, Pallas kernels for 2%

commit v1 on v0

--- a/solution.py
+++ b/solution.py
@@ -10,8 +10,12 @@
 AXES = ("y", "x", "z")
 RANK, CAP, SLOT_ROWS, WIDE = 32, 12, 16, 256
 PARAMS = pltpu.CompilerParams(vmem_limit_bytes=28 * 1024 * 1024)
+WHOLE = pltpu.CompilerParams(vmem_limit_bytes=62 * 1024 * 1024)
+LARGE = pltpu.CompilerParams(vmem_limit_bytes=103 * 512 * 1024)
 VMEM = pl.BlockSpec(memory_space=pltpu.VMEM)
 SMEM = pl.BlockSpec(memory_space=pltpu.SMEM)
+HBM = pl.BlockSpec(memory_space=pltpu.HBM)
+STEPS, TURN = 4, 128
 
 
 def mm(a, b):
@@ -32,53 +36,72 @@
     return jnp.concatenate([high, high, low], axis=0)
 
 
-def interp_kernel(modes_ref, index_ref, interp_ref, normals_ref, out_ref):
-    chunk = index_ref.shape[1]
-    nodes = modes_ref.shape[1]
-    rows = jnp.concatenate(
-        [
-            index_ref[...].astype(F32),
-            interp_ref[...],
-            normals_ref[...],
-            jnp.zeros((5, chunk), F32),
-        ],
-        axis=0,
-    )
-    columns = rows.T
+def interp_kernel(
+    modes_hbm, index_hbm, interp_hbm, normals_hbm, out_ref,
+    modes_ref, index_ref, interp_ref, normals_ref, sems,
+):
+    pairs = [
+        (index_hbm, index_ref), (interp_hbm, interp_ref), (normals_hbm, normals_ref),
+        (modes_hbm, modes_ref),
+    ]
+    copies = [
+        pltpu.make_async_copy(source, target, sems.at[number])
+        for number, (source, target) in enumerate(pairs)
+    ]
+    for copy in copies:
+        copy.start()
+    for copy in copies[:3]:
+        copy.wait()
+    slots, nodes = index_ref.shape[1], modes_ref.shape[1]
+    width = modes_ref.shape[2]
+    chunk = slots // STEPS
     node = lax.broadcasted_iota(I32, (chunk, nodes), 1).astype(F32)
-    mix = jnp.zeros((chunk, nodes), F32)
-    for corner in range(4):
-        here = columns[:, corner : corner + 1] == node
-        mix = mix + jnp.where(here, columns[:, 4 + corner : 5 + corner], 0.0)
-    table = jnp.concatenate([modes_ref[0], modes_ref[1], modes_ref[2]], axis=1)
-    high, low = halves(mix)
-    picked = mm(high, table) + mm(low, table)
-    width = modes_ref.shape[2]
-    velocity = jnp.zeros((chunk, width), F32)
-    for axis_id in range(3):
-        part = picked[:, axis_id * width : (axis_id + 1) * width]
-        velocity = velocity + columns[:, 8 + axis_id : 9 + axis_id] * part
-    pairs = velocity.reshape(chunk // 24, 24, width)
-    out_ref[:, 0:16, :] = pairs[:, 0:16, :].astype(BF16)
-    out_ref[:, 16:32, :] = pairs[:, 8:24, :].astype(BF16)
+    for step in range(STEPS):
+        lanes = slice(step * chunk, (step + 1) * chunk)
+        rows = jnp.concatenate(
+            [
+                index_ref[:, lanes].astype(F32),
+                interp_ref[:, lanes],
+                normals_ref[:, lanes],
+                jnp.zeros((5, chunk), F32),
+            ],
+            axis=0,
+        )
+        columns = rows.T
+        mix = jnp.zeros((chunk, nodes), F32)
+        for corner in range(4):
+            here = columns[:, corner : corner + 1] == node
+            mix = mix + jnp.where(here, columns[:, 4 + corner : 5 + corner], 0.0)
+        high, low = halves(mix)
+        if step == 0:
+            copies[3].wait()
+        table = jnp.concatenate([modes_ref[0], modes_ref[1], modes_ref[2]], axis=1)
+        picked = mm(high, table) + mm(low, table)
+        velocity = jnp.zeros((chunk, width), F32)
+        for axis_id in range(3):
+            part = picked[:, axis_id * width : (axis_id + 1) * width]
+            velocity = velocity + columns[:, 8 + axis_id : 9 + axis_id] * part
+        blocks = velocity.reshape(chunk // 24, 24, width)
+        where = slice(step * chunk // 24, (step + 1) * chunk // 24)
+        out_ref[where, 0:16, :] = blocks[:, 0:16, :].astype(BF16)
+        out_ref[where, 16:32, :] = blocks[:, 8:24, :].astype(BF16)
 
 
 def interpolate(node_modes, node_index, interp, normals):
     slots, width = node_index.shape[1], node_modes.shape[2]
-    steps = 4
-    chunk = slots // steps
     return pl.pallas_call(
         interp_kernel,
-        grid=(steps,),
-        in_specs=[
-            pl.BlockSpec(node_modes.shape, lambda i: (0, 0, 0)),
-            pl.BlockSpec((4, chunk), lambda i: (0, i)),
-            pl.BlockSpec((4, chunk), lambda i: (0, i)),
-            pl.BlockSpec((3, chunk), lambda i: (0, i)),
-        ],
-        out_specs=pl.BlockSpec((chunk // 24, 32, width), lambda i: (i, 0, 0)),
+        in_specs=[HBM] * 4,
+        out_specs=VMEM,
         out_shape=jax.ShapeDtypeStruct((slots // 24, 32, width), BF16),
-        compiler_params=PARAMS,
+        scratch_shapes=[
+            pltpu.VMEM(node_modes.shape, BF16),
+            pltpu.VMEM(node_index.shape, I32),
+            pltpu.VMEM(interp.shape, F32),
+            pltpu.VMEM(normals.shape, F32),
+            pltpu.SemaphoreType.DMA((4,)),
+        ],
+        compiler_params=WHOLE,
         cost_estimate=pl.CostEstimate(
             flops=2 * slots * 1024 * 384, bytes_accessed=1 << 20, transcendentals=0
         ),
@@ -138,9 +161,11 @@
 
 
 def solve_kernel(
-    arrived_ref, target_ref, diag_ref, right_ref, back_ref, mats_ref,
-    solved_ref, turned_ref, send_ref,
-):
+    arrived_ref, target_ref, diag_hbm, right_ref, back_ref, mats_ref,
+    solved_ref, turned_ref, send_ref, diag_ref, sem,
+):
+    fetch = pltpu.make_async_copy(diag_hbm, diag_ref, sem)
+    fetch.start()
     panels = diag_ref.shape[0]
     slots = target_ref.shape[1]
     step = 256
@@ -153,6 +178,7 @@
         parts.append(mm(pick, arrived))
     normal = jnp.concatenate(parts, axis=0)
     turned_ref[...] = normal.T.astype(BF16)
+    fetch.wait()
     solved = mm(diag_ref[...], normal.astype(BF16))
     solved_ref[...] = solved
     high, low = halves(solved)
@@ -168,14 +194,15 @@
     panels, width = diag.shape[0], arrived.shape[1]
     return pl.pallas_call(
         solve_kernel,
-        in_specs=[VMEM] * 6,
+        in_specs=[VMEM, VMEM, HBM, VMEM, VMEM, VMEM],
         out_specs=[VMEM] * 3,
+        scratch_shapes=[pltpu.VMEM(diag.shape, BF16), pltpu.SemaphoreType.DMA],
         out_shape=[
             jax.ShapeDtypeStruct((panels, width), F32),
             jax.ShapeDtypeStruct((width, panels), BF16),
             jax.ShapeDtypeStruct((peers, 4 * RANK, width), BF16),
         ],
-        compiler_params=PARAMS,
+        compiler_params=LARGE,
         cost_estimate=pl.CostEstimate(
             flops=1 << 30, bytes_accessed=4 << 20, transcendentals=0
         ),
@@ -192,24 +219,19 @@
 
     vectors = ref[position, 0 : 2 * RANK, :].astype(F32)
     ahead = jnp.concatenate([wide(0), wide(2)], axis=0)
-    return vectors[:RANK], vectors[RANK:], ahead, wide(1)
-
-
-def chain(ref, mine, first, last, lift):
-    count = ref.shape[0]
-    elements = [element(ref, position) for position in range(count)]
-    forward, own_forward, given = first, jnp.zeros_like(first), []
-    for position in range(count):
-        shift, gain, ahead, _ = elements[position]
-        own_forward = jnp.where(mine == position, forward, own_forward)
-        moved = mm(ahead, tall(forward))
-        given.append(lift(gain) - moved[RANK:])
-        forward = forward + moved[:RANK] + lift(shift)
-    backward, own_backward = last, jnp.zeros_like(last)
-    for position in reversed(range(count)):
-        own_backward = jnp.where(mine == position, backward, own_backward)
-        backward = backward + mm(elements[position][3], tall(backward)) + given[position]
-    return forward, backward, own_forward, own_backward
+    back = high[:, RANK : 2 * RANK].astype(F32) + low[:, RANK : 2 * RANK].astype(F32)
+    return vectors[:RANK], vectors[RANK:], ahead, back
+
+
+def gain_step(total, mask, middle):
+    factor = total[:, TURN : TURN + RANK]
+    if mask is not None:
+        factor = factor * mask
+    high, low = halves(factor)
+    middle_high, middle_low = halves(middle)
+    rows = factor.shape[0]
+    first = mm(jnp.concatenate([high, low], axis=0), middle_high)
+    return total + (first[:rows] + first[rows:] + mm(high, middle_low))
 
 
 def unit(offset):
@@ -220,26 +242,40 @@
 
 def inner_kernel(place_ref, got_ref, own_ref, send_ref):
     width = got_ref.shape[2]
+    mine = place_ref[0]
+    in_t, in_s = TURN, TURN + RANK
+    forward = unit(in_s)
+    own_s = jnp.zeros_like(forward)
+    total = jnp.concatenate([unit(in_t), unit(in_t)], axis=0)
     pad = jnp.zeros((RANK, WIDE - width), F32)
-    lift = lambda value: jnp.concatenate([value, pad], axis=1)
-    in_t, in_s = width, width + RANK
-    forward, backward, own_s, own_t = chain(
-        got_ref, place_ref[0], unit(in_s), unit(in_t), lift
-    )
-    own_ref[...] = jnp.concatenate([own_s, own_t], axis=0)
+    gap, tail = jnp.zeros((RANK, width), F32), jnp.zeros((RANK, WIDE - width - RANK), F32)
+    row = lax.broadcasted_iota(I32, (2 * RANK, RANK), 0)
+    for position in range(got_ref.shape[0]):
+        shift, gain, ahead, back = element(got_ref, position)
+        own_s = jnp.where(mine == position, forward, own_s)
+        moved = mm(ahead, tall(forward))
+        forward = forward + moved[:RANK] + jnp.concatenate([shift, pad], axis=1)
+        middle = (
+            jnp.concatenate([gain, pad], axis=1)
+            + jnp.concatenate([gap, back, tail], axis=1)
+            - moved[RANK:]
+        )
+        mask = jnp.where((row < RANK) | (position > mine), 1.0, 0.0)
+        total = gain_step(total, mask, middle)
+    own_ref[...] = jnp.concatenate([own_s, total[RANK:]], axis=0)
     eye = unit(0)[:, :RANK]
     mats = jnp.concatenate(
         [
             forward[:, in_s : in_s + RANK] - eye,
-            backward[:, in_t : in_t + RANK] - eye,
-            -backward[:, in_s : in_s + RANK],
+            total[:RANK, in_t : in_t + RANK] - eye,
+            -total[:RANK, in_s : in_s + RANK],
             jnp.zeros((RANK, RANK), F32),
         ],
         axis=1,
     )
     high, low = halves(mats)
     message = jnp.concatenate(
-        [forward[:, :width].astype(BF16), backward[:, :width].astype(BF16), high, low], axis=0
+        [forward[:, :width].astype(BF16), total[:RANK, :width].astype(BF16), high, low], axis=0
     )
     send_ref[...] = jnp.broadcast_to(message[None], send_ref.shape)
 
@@ -263,8 +299,18 @@
 ):
     width = got_ref.shape[2]
     panels = solved_ref.shape[0]
-    zero = jnp.zeros((RANK, width), F32)
-    _, _, in_s, in_t = chain(got_ref, place_ref[1], zero, zero, lambda value: value)
+    mine = place_ref[1]
+    forward = jnp.zeros((RANK, width), F32)
+    in_s, total = forward, unit(TURN)
+    rest = jnp.zeros((RANK, WIDE - width - RANK), F32)
+    for position in range(got_ref.shape[0]):
+        shift, gain, ahead, back = element(got_ref, position)
+        in_s = jnp.where(mine == position, forward, in_s)
+        moved = mm(ahead, tall(forward))
+        forward = forward + moved[:RANK] + shift
+        middle = jnp.concatenate([gain - moved[RANK:], back, rest], axis=1)
+        total = gain_step(total, jnp.where(position > mine, 1.0, 0.0), middle)
+    in_t = total[:, :width]
     own = own_ref[...]
     map_high, map_low = halves(own[:, width : width + 2 * RANK])
     maps = jnp.concatenate([map_high, map_low, map_high], axis=1)

time: 106 us -> 98.3 us (0.927)
  local copies, waits for them, and re-layouts: 6.54 us -> 1.61 us
  Pallas kernels: 21 us -> 18.6 us
    unnamed x24 -> x14, local copies, waits for them, and re-layouts: 6.54 us -> 1.61 us
    pallas_call x1, Pallas kernels: 5.97 us -> 4.4 us  [outer(): pl.pallas_call(outer_kernel, in_specs=[SMEM] + [VMEM] * 7, out_specs=[VME...]
where the time goes in v1:
time: 98.3 us; the launch traced here: 97.9 us
  blocking collectives  31.1 us (32%)
  waiting for transfers between devices  23 us (23%)
  starting transfers between devices  21.4 us (22%)
  Pallas kernels  18.6 us (19%)
  local copies, waits for them, and re-layouts  1.61 us (2%)
  between operations  1.4 us (1%)
    all_to_all x1, blocking collectives, body(): lax.all_to_all(mass.reshape(devices, rows, width), AXES, split_axis=0, co...  17.5 us
    all_to_all x1, starting transfers between devices, body(): lax.all_to_all(outgoing.reshape(devices, SLOT_ROWS, width), AXES, split_a...  15.4 us
    all_to_all x1, waiting for transfers between devices, body(): lax.all_to_all(outgoing.reshape(devices, SLOT_ROWS, width), AXES, split_a...  14.2 us
    all_to_all x1, blocking collectives, body(): got = lax.all_to_all(send, 'z', split_axis=0, concat_axis=0, tiled=True)  13.6 us
    all_to_all x1, waiting for transfers between devices, body(): lax.all_to_all(send, ('y', 'x'), split_axis=0, concat_axis=0, tiled=True)  7.33 us
    pallas_call x1, Pallas kernels, interpolate(): pl.pallas_call(interp_kernel, in_specs=[HBM] * 4, out_specs=VMEM, out_sha...  6.95 us
    all_to_all x1, starting transfers between devices, body(): lax.all_to_all(send, ('y', 'x'), split_axis=0, concat_axis=0, tiled=True)  5.92 us
    pallas_call x1, Pallas kernels, outer(): pl.pallas_call(outer_kernel, in_specs=[SMEM] + [VMEM] * 7, out_specs=[VME...  4.4 us
  transfers between devices with their start and end apart: 3, of which 3 were waited for; matrix products, arithmetic and copies ran while one was open for 0% of the time, Pallas kernels for 2%

profile of v1, /device:TPU:2, one launch (start us, length us, event | category | flops | bytes accessed | tf_op | source)
XLA Modules:
  0.0 97.9 jit_solution(8112242000584477231)
XLA Ops:
  0.6 0.0 copy-start.5
  0.6 0.0 copy-start.4
  0.7 0.0 copy-start.6
  0.7 0.0 copy-start.2
  0.7 0.0 copy-start.3
  0.7 7.0 %shard_map.131 = bf16[64,32,128]{2,1,0:T(8,128)(2,1)} custom-call(bf16[3,1024,128]{2,1,0:T(8,128)(2,1)} %modes_hbm.1, s32[4,1536]{1,0:T(4,128)} %index_hbm.1, f32[4,1536]{1,0:T(4,128)} %interp_hbm.1, f32[3,1536]{1,0:T(4,128)} %normals_hbm.1), custom_call_target="tpu_custom_call" | custom-call | flops 1207959552 | bytes 1048576 | tf_op jit(solution)/shard_map/pallas_call | solution.py:92
  7.6 15.4 %all-to-all-start = ((bf16[128,16,128]{2,1,0:T(8,128)(2,1)}), bf16[128,16,128]{2,1,0:T(8,128)(2,1)S(1)}, u32[]{:S(2)}, u32[]{:S(2)}) async-start(bf16[128,16,128]{2,1,0:T(8,128)(2,1)} %bitcast.23), calls=%async_computation | async-start | bytes 1048576 | tf_op jit(solution)/shard_map/all_to_all | solution.py:357
  23.8 0.1 pad_add_fusion.place_ref
  23.8 0.0 copy-done.5
  23.8 0.0 copy-done.4
  23.8 0.0 copy-done.6
  23.8 0.0 copy-done.2
  23.9 0.0 copy-done.3
  23.9 0.0 copy-start.1
  23.9 1.6 %copy-done.1 = bf16[1024,1024]{1,0:T(8,128)(2,1)S(1)} copy-done((bf16[1024,1024]{1,0:T(8,128)(2,1)S(1)}, bf16[1024,1024]{1,0:T(8,128)(2,1)}, u32[]{:S(2)}) %copy-start.1) | copy-done | bytes 2097176
  25.5 1.8 %shard_map.132 = (bf16[1024,128]{1,0:T(8,128)(2,1)S(1)}, bf16[64,128]{1,0:T(8,128)(2,1)S(1)}, f32[1,2048]{1,0:T(1,128)S(1)}) custom-call(s32[4]{0:T(128)S(1)} %pad_add_fusion.place_ref, s32[1]{0:T(128)S(6)} %copy.14.rank_ref, s32[1,128]{1,0:T(1,128)S(1)} %bitcast.22, bf16[1024,1024]{1,0:T(8,128)(2,1)S(1)} %copy-done.1, bf16[32,1024]{1,0:T(8,128)(2,1)S(1)} %bitcast.16, ...), custom_call_target="tpu_custom_call" | custom-call | flops 4294967296 | bytes 8388608 | tf_op jit(solution)/shard_map/pallas_call | solution.py:147
  27.2 14.2 %all-to-all-done = bf16[128,16,128]{2,1,0:T(8,128)(2,1)S(1)} async-done(((bf16[128,16,128]{2,1,0:T(8,128)(2,1)}), bf16[128,16,128]{2,1,0:T(8,128)(2,1)S(1)}, u32[]{:S(2)}, u32[]{:S(2)}) %all-to-all-start) | async-done | bytes 524320 | tf_op jit(solution)/shard_map/all_to_all | solution.py:357
  41.4 0.0 copy-start
  41.4 2.5 %shard_map.133 = (f32[1024,128]{1,0:T(8,128)S(1)}, bf16[128,1024]{1,0:T(8,128)(2,1)S(1)}, bf16[8,128,128]{2,1,0:T(8,128)(2,1)S(1)}) custom-call(bf16[2048,128]{1,0:T(8,128)(2,1)S(1)} %bitcast.13, f32[1,2048]{1,0:T(1,128)S(1)} %get-tuple-element.12.target_ref, bf16[1024,1024]{1,0:T(8,128)(2,1)} %diag_hbm.1, bf16[32,1024]{1,0:T(8,128)(2,1)S(1)} %bitcast.19, ...), custom_call_target="tpu_custom_call" | custom-call | flops 1073741824 | bytes 4194304 | tf_op jit(solution)/shard_map/pallas_call | solution.py:195
  44.0 13.6 %all_to_all.20.got_ref = bf16[8,128,128]{2,1,0:T(8,128)(2,1)S(1)} all-to-all(bf16[8,128,128]{2,1,0:T(8,128)(2,1)S(1)} %get-tuple-element.14), channel_id=1, replica_groups=mesh['side'=2,'y'=4,'x'=4,'z'=8] {'z'}, dimensions={0} | all-to-all | bytes 524288 | tf_op jit(solution)/shard_map/all_to_all | solution.py:369
  57.6 2.9 %shard_map.134 = (f32[64,256]{1,0:T(8,128)S(1)}, bf16[16,128,128]{2,1,0:T(8,128)(2,1)}) custom-call(s32[4]{0:T(128)S(1)} %pad_add_fusion.place_ref, bf16[8,128,128]{2,1,0:T(8,128)(2,1)S(1)} %all_to_all.20.got_ref), custom_call_target="tpu_custom_call" | custom-call | tf_op jit(solution)/shard_map/pallas_call | solution.py:284
  60.5 5.9 %all-to-all-start.2 = ((bf16[16,128,128]{2,1,0:T(8,128)(2,1)}), bf16[16,128,128]{2,1,0:T(8,128)(2,1)S(1)}, u32[]{:S(2)}, u32[]{:S(2)}) async-start(bf16[16,128,128]{2,1,0:T(8,128)(2,1)} %get-tuple-element.15), calls=%async_computation.2 | async-start | bytes 1048576 | tf_op jit(solution)/shard_map/all_to_all | solution.py:371
  66.4 0.0 collective-permute-start
  66.4 1.5 %collective-permute-done.other_ref = bf16[128,1024]{1,0:T(8,128)(2,1)S(1)} collective-permute-done((bf16[128,1024]{1,0:T(8,128)(2,1)S(1)}, bf16[128,1024]{1,0:T(8,128)(2,1)S(1)}, u32[]{:S(2)}, u32[]{:S(2)}) %collective-permute-start) | collective-permute-done | bytes 262176 | tf_op jit(solution)/shard_map/ppermute | solution.py:368
  68.0 7.3 %all-to-all-done.2.got_ref = bf16[16,128,128]{2,1,0:T(8,128)(2,1)S(1)} async-done(((bf16[16,128,128]{2,1,0:T(8,128)(2,1)}), bf16[16,128,128]{2,1,0:T(8,128)(2,1)S(1)}, u32[]{:S(2)}, u32[]{:S(2)}) %all-to-all-start.2) | async-done | bytes 524320 | tf_op jit(solution)/shard_map/all_to_all | solution.py:371
  75.3 0.0 copy-done
  75.3 4.4 %shard_map.135 = (bf16[1024,128]{1,0:T(8,128)(2,1)}, f32[256,128]{1,0:T(8,128)S(1)}) custom-call(s32[4]{0:T(128)S(1)} %pad_add_fusion.place_ref, bf16[16,128,128]{2,1,0:T(8,128)(2,1)S(1)} %all-to-all-done.2.got_ref, f32[64,256]{1,0:T(8,128)S(1)} %get-tuple-element.16.own_ref, f32[1024,128]{1,0:T(8,128)S(1)} %get-tuple-element.17.solved_ref, ...), custom_call_target="tpu_custom_call" | custom-call | tf_op jit(solution)/shard_map/pallas_call | solution.py:336
  79.7 17.5 %all_to_all.21 = f32[128,2,128]{2,1,0:T(2,128)S(1)} all-to-all(f32[128,2,128]{2,1,0:T(2,128)S(1)} %bitcast.14), channel_id=1, replica_groups=mesh['side'=2,'y'=4,'x'=4,'z'=8] {'y','x','z'}, dimensions={0} | all-to-all | bytes 262144 | tf_op jit(solution)/shard_map/all_to_all | solution.py:376
  97.2 0.7 reduce_sum.9
Async XLA Ops:
  0.6 23.2 %copy-start.5 = (bf16[1024,32]{0,1:T(8,128)(2,1)S(1)}, bf16[1024,32]{0,1:T(8,128)(2,1)}, u32[]{:S(2)}) copy-start(bf16[1024,32]{0,1:T(8,128)(2,1)} %param.21) | copy-start | bytes 196612
  0.6 23.2 %copy-start.4 = (bf16[1024,32]{0,1:T(8,128)(2,1)S(1)}, bf16[1024,32]{0,1:T(8,128)(2,1)}, u32[]{:S(2)}) copy-start(bf16[1024,32]{0,1:T(8,128)(2,1)} %param.19) | copy-start | bytes 196612
  0.7 23.2 %copy-start.6 = (s32[128,1]{0,1:T(1,128)S(1)}, s32[128,1]{0,1:T(1,128)}, u32[]{:S(2)}) copy-start(s32[128,1]{0,1:T(1,128)} %param.16) | copy-start | bytes 1540
  0.7 23.2 %copy-start.2 = (bf16[1024,32]{0,1:T(8,128)(2,1)S(1)}, bf16[1024,32]{0,1:T(8,128)(2,1)}, u32[]{:S(2)}) copy-start(bf16[1024,32]{0,1:T(8,128)(2,1)} %param.18) | copy-start | bytes 196612
  0.7 23.2 %copy-start.3 = (bf16[1024,32]{0,1:T(8,128)(2,1)S(1)}, bf16[1024,32]{0,1:T(8,128)(2,1)}, u32[]{:S(2)}) copy-start(bf16[1024,32]{0,1:T(8,128)(2,1)} %param.20) | copy-start | bytes 196612
  7.6 33.8 %all-to-all-start = ((bf16[128,16,128]{2,1,0:T(8,128)(2,1)}), bf16[128,16,128]{2,1,0:T(8,128)(2,1)S(1)}, u32[]{:S(2)}, u32[]{:S(2)}) async-start(bf16[128,16,128]{2,1,0:T(8,128)(2,1)} %bitcast.23), calls=%async_computation | async-start | bytes 1048576 | tf_op jit(solution)/shard_map/all_to_all | solution.py:357
  23.9 1.6 %copy-start.1 = (bf16[1024,1024]{1,0:T(8,128)(2,1)S(1)}, bf16[1024,1024]{1,0:T(8,128)(2,1)}, u32[]{:S(2)}) copy-start(bf16[1024,1024]{1,0:T(8,128)(2,1)} %diag_hbm.1) | copy-start | bytes 6291460
  41.4 33.9 %copy-start = (f32[1024]{0:T(1024)S(1)}, f32[1024]{0:T(1024)}, u32[]{:S(2)}) copy-start(f32[1024]{0:T(1024)} %param.23) | copy-start | bytes 12292
  60.5 14.8 %all-to-all-start.2 = ((bf16[16,128,128]{2,1,0:T(8,128)(2,1)}), bf16[16,128,128]{2,1,0:T(8,128)(2,1)S(1)}, u32[]{:S(2)}, u32[]{:S(2)}) async-start(bf16[16,128,128]{2,1,0:T(8,128)(2,1)} %get-tuple-element.15), calls=%async_computation.2 | async-start | bytes 1048576 | tf_op jit(solution)/shard_map/all_to_all | solution.py:371
  66.4 1.5 %collective-permute-start = (bf16[128,1024]{1,0:T(8,128)(2,1)S(1)}, bf16[128,1024]{1,0:T(8,128)(2,1)S(1)}, u32[]{:S(2)}, u32[]{:S(2)}) collective-permute-start(bf16[128,1024]{1,0:T(8,128)(2,1)S(1)} %get-tuple-element.19.turned_ref), channel_id=1, source_target_pairs={{0,128},{128,0},{1,129},{129,1},{2,130},{130,2},{3,131},{131,3},{4... | collective-permute-start | bytes 786440 | tf_op jit(solution)/shard_map/ppermute | solution.py:368

commit v2 on v1

--- a/solution.py
+++ b/solution.py
@@ -11,7 +11,6 @@
 RANK, CAP, SLOT_ROWS, WIDE = 32, 12, 16, 256
 PARAMS = pltpu.CompilerParams(vmem_limit_bytes=28 * 1024 * 1024)
 WHOLE = pltpu.CompilerParams(vmem_limit_bytes=62 * 1024 * 1024)
-LARGE = pltpu.CompilerParams(vmem_limit_bytes=103 * 512 * 1024)
 VMEM = pl.BlockSpec(memory_space=pltpu.VMEM)
 SMEM = pl.BlockSpec(memory_space=pltpu.SMEM)
 HBM = pl.BlockSpec(memory_space=pltpu.HBM)
@@ -109,8 +108,8 @@
 
 
 def prepare_kernel(
-    place_ref, rank_ref, count_ref, diag_ref, lower_ref, right_ref, upper_ref, back_ref,
-    stack_ref, mats_ref, target_ref,
+    place_ref, rank_ref, count_ref, diag_ref, lower_ref, right_ref, upper_ref, back_ref, area_ref,
+    stack_ref, mats_ref, target_ref, scaled_ref, area_out_ref,
 ):
     panels = diag_ref.shape[0]
     keep = lax.broadcasted_iota(I32, (RANK, panels), 0) < rank_ref[0]
@@ -127,9 +126,17 @@
     mats = jnp.concatenate([-seen[:RANK], -back, seen[RANK:], blank], axis=1)
     mats_high, mats_low = halves(mats)
     mats_ref[...] = jnp.concatenate([mats_high, mats_low], axis=0)
+    upper_left = upper.astype(F32).T
     stack_ref[...] = jnp.concatenate(
-        [high, upper.astype(F32).T.astype(BF16), low, jnp.zeros((panels, RANK), BF16)], axis=1
-    )
+        [high, upper_left.astype(BF16), low, jnp.zeros((panels, RANK), BF16)], axis=1
+    )
+    area = jnp.broadcast_to(jnp.broadcast_to(area_ref[...], (8, panels)).T[:, 0:1], (panels, 128))
+    area_out_ref[...] = area
+    gap = jnp.zeros((panels, 3 * RANK), F32)
+    minus = -area[:, :RANK]
+    scaled_ref[...] = jnp.concatenate(
+        [gap, minus * spread, gap, minus * upper_left], axis=1
+    ).astype(BF16)
     sources = count_ref.shape[1]
     slots = target_ref.shape[1]
     counts = jnp.broadcast_to(count_ref[...].astype(F32), (16, sources)).astype(BF16)
@@ -142,31 +149,28 @@
     target_ref[...] = jnp.where((slot >= 0.0) & (slot < mine), start + slot, -1.0)
 
 
-def prepare(place, rank, count, diag, lower, right, upper, back):
+def prepare(place, rank, count, diag, lower, right, upper, back, area):
     panels, slots = diag.shape[0], count.shape[1] * SLOT_ROWS
     return pl.pallas_call(
         prepare_kernel,
-        in_specs=[SMEM, SMEM] + [VMEM] * 6,
-        out_specs=[VMEM] * 3,
+        in_specs=[SMEM, SMEM] + [VMEM] * 7,
+        out_specs=[VMEM] * 5,
         out_shape=[
             jax.ShapeDtypeStruct((panels, 4 * RANK), BF16),
             jax.ShapeDtypeStruct((2 * RANK, 4 * RANK), BF16),
             jax.ShapeDtypeStruct((1, slots), F32),
+            jax.ShapeDtypeStruct((panels, 8 * RANK), BF16),
+            jax.ShapeDtypeStruct((panels, 4 * RANK), F32),
         ],
         compiler_params=PARAMS,
         cost_estimate=pl.CostEstimate(
             flops=4 << 30, bytes_accessed=8 << 20, transcendentals=0
         ),
-    )(place, rank, count, diag, lower, right, upper, back)
-
-
-def solve_kernel(
-    arrived_ref, target_ref, diag_hbm, right_ref, back_ref, mats_ref,
-    solved_ref, turned_ref, send_ref, diag_ref, sem,
-):
-    fetch = pltpu.make_async_copy(diag_hbm, diag_ref, sem)
-    fetch.start()
-    panels = diag_ref.shape[0]
+    )(place, rank, count, diag, lower, right, upper, back, area)
+
+
+def select_kernel(arrived_ref, target_ref, normal_ref, turned_ref):
+    panels, width = normal_ref.shape
     slots = target_ref.shape[1]
     step = 256
     target = target_ref[...]
@@ -175,38 +179,101 @@
     for begin in range(0, panels, step):
         panel = (lax.broadcasted_iota(I32, (step, slots), 0) + begin).astype(F32)
         pick = jnp.where(panel == target, 1.0, 0.0).astype(BF16)
-        parts.append(mm(pick, arrived))
+        parts.append(mm(pick, arrived).astype(BF16))
     normal = jnp.concatenate(parts, axis=0)
-    turned_ref[...] = normal.T.astype(BF16)
-    fetch.wait()
-    solved = mm(diag_ref[...], normal.astype(BF16))
+    normal_ref[...] = normal
+    row = lax.broadcasted_iota(I32, (width, width), 0)
+    mode = (row % 16) // 2 * 16 + row // 16 * 2 + row % 2
+    order = jnp.where(lax.broadcasted_iota(I32, (width, width), 1) == mode, 1.0, 0.0)
+    turned_ref[...] = mm_t(order.astype(BF16), normal).astype(BF16)
+
+
+def select(arrived, target, panels):
+    width = arrived.shape[1]
+    return pl.pallas_call(
+        select_kernel,
+        in_specs=[VMEM] * 2,
+        out_specs=[VMEM] * 2,
+        out_shape=[
+            jax.ShapeDtypeStruct((panels, width), BF16),
+            jax.ShapeDtypeStruct((width, panels), BF16),
+        ],
+        compiler_params=PARAMS,
+        cost_estimate=pl.CostEstimate(
+            flops=1 << 29, bytes_accessed=2 << 20, transcendentals=0
+        ),
+    )(arrived, target)
+
+
+def solve_kernel(normal_ref, diag_ref, right_ref, back_ref, solved_ref, seen_ref):
+    solved = mm(diag_ref[...], normal_ref[...])
     solved_ref[...] = solved
     high, low = halves(solved)
     width = solved.shape[1]
     both = jnp.concatenate([right_ref[...], back_ref[...]], axis=0)
     seen = mm(both, jnp.concatenate([high, low], axis=1))
-    seen = (seen[:, :width] + seen[:, width:]).astype(BF16)
-    message = jnp.concatenate([seen, mats_ref[...]], axis=0)
-    send_ref[...] = jnp.broadcast_to(message[None], send_ref.shape)
-
-
-def solve(arrived, target, diag, right, back, mats, peers):
-    panels, width = diag.shape[0], arrived.shape[1]
+    seen_ref[...] = (seen[:, :width] + seen[:, width:]).astype(BF16)
+
+
+def solve(normal, diag, right, back):
+    panels, width = normal.shape
     return pl.pallas_call(
         solve_kernel,
-        in_specs=[VMEM, VMEM, HBM, VMEM, VMEM, VMEM],
-        out_specs=[VMEM] * 3,
-        scratch_shapes=[pltpu.VMEM(diag.shape, BF16), pltpu.SemaphoreType.DMA],
+        in_specs=[VMEM] * 4,
+        out_specs=[VMEM] * 2,
         out_shape=[
             jax.ShapeDtypeStruct((panels, width), F32),
-            jax.ShapeDtypeStruct((width, panels), BF16),
-            jax.ShapeDtypeStruct((peers, 4 * RANK, width), BF16),
-        ],
-        compiler_params=LARGE,
+            jax.ShapeDtypeStruct((2 * RANK, width), BF16),
+        ],
+        compiler_params=PARAMS,
         cost_estimate=pl.CostEstimate(
-            flops=1 << 30, bytes_accessed=4 << 20, transcendentals=0
+            flops=1 << 29, bytes_accessed=4 << 20, transcendentals=0
         ),
-    )(arrived, target, diag, right, back, mats)
+    )(normal, diag, right, back)
+
+
+def local_kernel(
+    place_ref, solved_ref, scaled_ref, area_ref, turned_ref, other_ref, seen_ref, mats_ref,
+    send_ref,
+):
+    width = solved_ref.shape[1]
+    peers = send_ref.shape[0]
+    part = width // peers
+    weighted = (area_ref[...] * solved_ref[...]).astype(BF16)
+    factor = jnp.concatenate([weighted, scaled_ref[...]], axis=1)
+    own = mm(turned_ref[...], factor)
+    other = mm(other_ref[...], factor)
+    even = place_ref[2] == 0
+    send_ref[:, 0 : 2 * RANK, :] = jnp.broadcast_to(
+        seen_ref[...][None], (peers, 2 * RANK, width)
+    )
+    mats = mats_ref[...].astype(F32)
+    for side in range(2):
+        rows = jnp.where(even, other, own) if side else jnp.where(even, own, other)
+        high, low = halves(rows[:, :width])
+        begin = 4 * RANK + side * part
+        send_ref[:, begin : begin + part, :] = high.reshape(peers, part, width)
+        begin = begin + RANK
+        send_ref[:, begin : begin + part, :] = low.reshape(peers, part, width)
+        for which in range(2):
+            begin = which * RANK + side * part
+            block = rows[:, (1 + which) * width : (2 + which) * width].reshape(peers, part, width)
+            block = (block + mats[begin : begin + part][None]).astype(BF16)
+            send_ref[:, 2 * RANK + begin : 2 * RANK + begin + part, :] = block
+
+
+def local(place, solved, scaled, area, turned, other, seen, mats, peers):
+    width = solved.shape[1]
+    return pl.pallas_call(
+        local_kernel,
+        in_specs=[SMEM] + [VMEM] * 7,
+        out_specs=VMEM,
+        out_shape=jax.ShapeDtypeStruct((peers, 6 * RANK, width), BF16),
+        compiler_params=PARAMS,
+        cost_estimate=pl.CostEstimate(
+            flops=1 << 28, bytes_accessed=2 << 20, transcendentals=0
+        ),
+    )(place, solved, scaled, area, turned, other, seen, mats)
 
 
 def element(ref, position):
@@ -218,9 +285,8 @@
         return jnp.concatenate([high[:, lanes], low[:, lanes], high[:, lanes]], axis=1)
 
     vectors = ref[position, 0 : 2 * RANK, :].astype(F32)
-    ahead = jnp.concatenate([wide(0), wide(2)], axis=0)
     back = high[:, RANK : 2 * RANK].astype(F32) + low[:, RANK : 2 * RANK].astype(F32)
-    return vectors[:RANK], vectors[RANK:], ahead, back
+    return vectors[:RANK], vectors[RANK:], [wide(0), wide(2)], back
 
 
 def gain_step(total, mask, middle):
@@ -246,23 +312,34 @@
     in_t, in_s = TURN, TURN + RANK
     forward = unit(in_s)
     own_s = jnp.zeros_like(forward)
-    total = jnp.concatenate([unit(in_t), unit(in_t)], axis=0)
+    total = jnp.concatenate([unit(in_t), unit(in_t), jnp.zeros((RANK, WIDE), F32)], axis=0)
     pad = jnp.zeros((RANK, WIDE - width), F32)
     gap, tail = jnp.zeros((RANK, width), F32), jnp.zeros((RANK, WIDE - width - RANK), F32)
-    row = lax.broadcasted_iota(I32, (2 * RANK, RANK), 0)
+    none = jnp.zeros((2 * RANK, WIDE), F32)
+    blank = jnp.zeros((RANK, RANK), BF16)
+    row = lax.broadcasted_iota(I32, (3 * RANK, RANK), 0)
+    middle_rows = (row >= RANK) & (row < 2 * RANK)
     for position in range(got_ref.shape[0]):
         shift, gain, ahead, back = element(got_ref, position)
+        by_s = got_ref[position, 2 * RANK : 3 * RANK, 3 * RANK : 4 * RANK]
+        by_t = got_ref[position, 3 * RANK : 4 * RANK, 3 * RANK : 4 * RANK].astype(F32)
+        fixed = got_ref[position, 4 * RANK : 5 * RANK, :].astype(F32)
+        fixed = fixed + got_ref[position, 5 * RANK : 6 * RANK, :].astype(F32)
+        ahead = jnp.concatenate(
+            ahead + [jnp.concatenate([by_s, blank, by_s], axis=1)], axis=0
+        )
         own_s = jnp.where(mine == position, forward, own_s)
         moved = mm(ahead, tall(forward))
         forward = forward + moved[:RANK] + jnp.concatenate([shift, pad], axis=1)
         middle = (
             jnp.concatenate([gain, pad], axis=1)
             + jnp.concatenate([gap, back, tail], axis=1)
-            - moved[RANK:]
+            - moved[RANK : 2 * RANK]
         )
-        mask = jnp.where((row < RANK) | (position > mine), 1.0, 0.0)
-        total = gain_step(total, mask, middle)
-    own_ref[...] = jnp.concatenate([own_s, total[RANK:]], axis=0)
+        mask = jnp.where(middle_rows & (position <= mine), 0.0, 1.0)
+        mass = moved[2 * RANK :] + jnp.concatenate([fixed, by_t, tail], axis=1)
+        total = gain_step(total, mask, middle) + jnp.concatenate([none, mass], axis=0)
+    own_ref[...] = jnp.concatenate([own_s, total[RANK : 2 * RANK]], axis=0)
     eye = unit(0)[:, :RANK]
     mats = jnp.concatenate(
         [
@@ -277,7 +354,20 @@
     message = jnp.concatenate(
         [forward[:, :width].astype(BF16), total[:RANK, :width].astype(BF16), high, low], axis=0
     )
-    send_ref[...] = jnp.broadcast_to(message[None], send_ref.shape)
+    peers = send_ref.shape[0]
+    send_ref[:, 0 : 4 * RANK, :] = jnp.broadcast_to(message[None], (peers, 4 * RANK, width))
+    mass = total[2 * RANK :]
+    fixed_high, fixed_low = halves(mass[:, :width])
+    by_s_high, by_s_low = halves(mass[:, in_s : in_s + RANK])
+    by_t_high, by_t_low = halves(mass[:, in_t : in_t + RANK])
+    maps = jnp.concatenate([by_s_high, by_s_low, by_t_high, by_t_low], axis=1)
+    sources = jnp.concatenate([fixed_high, fixed_low, maps, jnp.zeros_like(maps)], axis=0)
+    row = lax.broadcasted_iota(I32, (peers * 16, 4 * RANK), 0)
+    column = lax.broadcasted_iota(I32, (peers * 16, 4 * RANK), 1)
+    slot = row % 16
+    block = jnp.where(slot < 4, slot // 2, jnp.where((slot == 8) | (slot == 9), 2, 3))
+    pick = jnp.where(column == block * RANK + row // 16 * 2 + slot % 2, 1.0, 0.0).astype(BF16)
+    send_ref[:, 4 * RANK :, :] = mm(pick, sources).astype(BF16).reshape(peers, 16, width)
 
 
 def inner(place, got, peers):
@@ -287,30 +377,44 @@
         out_specs=[VMEM] * 2,
         out_shape=[
             jax.ShapeDtypeStruct((2 * RANK, WIDE), F32),
-            jax.ShapeDtypeStruct((peers,) + got.shape[1:], BF16),
+            jax.ShapeDtypeStruct((peers, 4 * RANK + 16, got.shape[2]), BF16),
         ],
         compiler_params=PARAMS,
     )(place, got)
 
 
 def outer_kernel(
-    place_ref, got_ref, own_ref, solved_ref, stack_ref, turned_ref, other_ref, area_ref,
-    potential_ref, mass_ref,
+    place_ref, got_ref, own_ref, solved_ref, stack_ref, potential_ref, mass_ref,
 ):
     width = got_ref.shape[2]
-    panels = solved_ref.shape[0]
     mine = place_ref[1]
     forward = jnp.zeros((RANK, width), F32)
-    in_s, total = forward, unit(TURN)
+    in_s = forward
+    total = jnp.concatenate([unit(TURN), jnp.zeros((16, WIDE), F32)], axis=0)
     rest = jnp.zeros((RANK, WIDE - width - RANK), F32)
+    none, low_rest = jnp.zeros((RANK, WIDE), F32), jnp.zeros((16, WIDE - width - RANK), F32)
+    zero8, zero16 = jnp.zeros((8, 4 * RANK), F32), jnp.zeros((16, RANK), BF16)
+    row = lax.broadcasted_iota(I32, (RANK + 16, RANK), 0)
     for position in range(got_ref.shape[0]):
         shift, gain, ahead, back = element(got_ref, position)
+        fixed = got_ref[position, 4 * RANK :, :].astype(F32)
+        maps = jnp.concatenate([fixed[8:16], zero8], axis=0)
+        by_s_high = maps[:, :RANK].astype(BF16)
+        by_s_low = maps[:, RANK : 2 * RANK].astype(BF16)
+        by_t = maps[:, 2 * RANK : 3 * RANK] + maps[:, 3 * RANK :]
+        ahead = jnp.concatenate(
+            ahead + [jnp.concatenate([by_s_high, by_s_low, by_s_high], axis=1)], axis=0
+        )
         in_s = jnp.where(mine == position, forward, in_s)
         moved = mm(ahead, tall(forward))
         forward = forward + moved[:RANK] + shift
-        middle = jnp.concatenate([gain - moved[RANK:], back, rest], axis=1)
-        total = gain_step(total, jnp.where(position > mine, 1.0, 0.0), middle)
-    in_t = total[:, :width]
+        middle = jnp.concatenate([gain - moved[RANK : 2 * RANK], back, rest], axis=1)
+        mask = jnp.where((row < RANK) & (position <= mine), 0.0, 1.0)
+        mass = jnp.concatenate([fixed + moved[2 * RANK :], by_t, low_rest], axis=1)
+        total = gain_step(total, mask, middle) + jnp.concatenate([none, mass], axis=0)
+    in_t = total[:RANK, :width]
+    mass = total[RANK:, :width]
+    mass_ref[...] = mass[0:2] + mass[2:4]
     own = own_ref[...]
     map_high, map_low = halves(own[:, width : width + 2 * RANK])
     maps = jnp.concatenate([map_high, map_low, map_high], axis=1)
@@ -320,29 +424,22 @@
     left = jnp.concatenate([high, high[:RANK], blank], axis=0)
     right = jnp.concatenate([low, blank, blank], axis=0)
     fixed = mm(stack_ref[...], jnp.concatenate([left, right], axis=1))
-    potential = (solved_ref[...] - (fixed[:, :width] + fixed[:, width:])).astype(BF16)
-    potential_ref[...] = potential
-    area = jnp.broadcast_to(area_ref[...], (8, panels)).T[:, 0:1]
-    weighted = (area * potential.astype(F32)).astype(BF16)
-    side = place_ref[2]
-    mass_ref[pl.ds(pl.multiple_of(side * width, width), width), :] = mm(turned_ref[...], weighted)
-    mass_ref[pl.ds(pl.multiple_of((1 - side) * width, width), width), :] = mm(
-        other_ref[...], weighted
-    )
-
-
-def outer(place, got, own, solved, stack, turned, other, area):
+    potential = solved_ref[...] - (fixed[:, :width] + fixed[:, width:])
+    potential_ref[...] = potential.astype(BF16)
+
+
+def outer(place, got, own, solved, stack):
     panels, width = solved.shape
     return pl.pallas_call(
         outer_kernel,
-        in_specs=[SMEM] + [VMEM] * 7,
+        in_specs=[SMEM] + [VMEM] * 4,
         out_specs=[VMEM] * 2,
         out_shape=[
             jax.ShapeDtypeStruct((panels, width), BF16),
-            jax.ShapeDtypeStruct((2 * width, width), F32),
-        ],
-        compiler_params=PARAMS,
-    )(place, got, own, solved, stack, turned, other, area)
+            jax.ShapeDtypeStruct((2, width), F32),
+        ],
+        compiler_params=PARAMS,
+    )(place, got, own, solved, stack)
 
 
 def body(
@@ -358,25 +455,18 @@
         outgoing.reshape(devices, SLOT_ROWS, width), AXES, split_axis=0, concat_axis=0, tiled=True
     ).reshape(devices * SLOT_ROWS, width)
     right, back = lower_right.T, upper_right.T
-    stack, mats, target = prepare(
+    stack, mats, target, scaled, area = prepare(
         place, ranks, counts.reshape(1, devices), inverse_diag, lower_left.T, right,
-        upper_left.T, back,
-    )
-    solved, turned, send = solve(
-        arrived, target, inverse_diag, right, back, mats, inner_size
-    )
+        upper_left.T, back, areas.reshape(1, -1),
+    )
+    normal, turned = select(arrived, target, inverse_diag.shape[0])
     other = lax.ppermute(turned, "side", [(0, 1), (1, 0)])
+    solved, seen = solve(normal, inverse_diag, right, back)
+    send = local(place, solved, scaled, area, turned, other, seen, mats, inner_size)
     got = lax.all_to_all(send, "z", split_axis=0, concat_axis=0, tiled=True)
     own, send = inner(place, got, outer_size)
     got = lax.all_to_all(send, ("y", "x"), split_axis=0, concat_axis=0, tiled=True)
-    potentials, mass = outer(
-        place, got, own, solved, stack, turned, other, areas.reshape(1, -1)
-    )
-    rows = mass.shape[0] // devices
-    pieces = lax.all_to_all(
-        mass.reshape(devices, rows, width), AXES, split_axis=0, concat_axis=0, tiled=True
-    )
-    return potentials, jnp.sum(pieces, axis=0)
+    return outer(place, got, own, solved, stack)
 
 
 def solution(mesh):

time: 98.3 us -> 88.6 us (0.901)
  waiting for transfers between devices: 23 us -> 9.74 us
  starting transfers between devices: 21.4 us -> 15.5 us
  local copies, waits for them, and re-layouts: 1.61 us -> 7.22 us
  blocking collectives: 31.1 us -> 34.7 us
    all_to_all x1 -> x0, waiting for transfers between devices: 7.33 us -> none  [body(): lax.all_to_all(send, ('y', 'x'), split_axis=0, concat_axis=0, tiled=True)]
    all_to_all x1 -> x0, starting transfers between devices: 5.92 us -> none  [body(): lax.all_to_all(send, ('y', 'x'), split_axis=0, concat_axis=0, tiled=True)]
    unnamed x14 -> x28, local copies, waits for them, and re-layouts: 1.61 us -> 7.22 us
    all_to_all x1, waiting for transfers between devices: 14.2 us -> 9.15 us  [body(): lax.all_to_all(outgoing.reshape(devices, SLOT_ROWS, width), AXES, split_a...]
    all_to_all x1, blocking collectives: 13.6 us -> 18.1 us  [body(): got = lax.all_to_all(send, 'z', split_axis=0, concat_axis=0, tiled=True)]
    pallas_call x3 -> x5, Pallas kernels: 8.73 us -> 9.43 us  [the longest x1 4.22 us: outer(): pl.pallas_call(outer_kernel, in_specs=[SMEM] + [VMEM] * 4, out_specs=[VME...]
  transfers between devices with their start and end apart: 3 -> 2, of which waited for: 3 -> 2; matrix products, arithmetic and copies ran while one was open for 0% -> 0% of each run, Pallas kernels for 2% -> 3%
where the time goes in v2:
time: 88.6 us; the launch traced here: 87.4 us
  blocking collectives  34.7 us (39%)
  Pallas kernels  18.7 us (21%)
  starting transfers between devices  15.5 us (17%)
  waiting for transfers between devices  9.74 us (11%)
  local copies, waits for them, and re-layouts  7.22 us (8%)
  between operations  1.4 us (2%)
    all_to_all x1, blocking collectives, body(): got = lax.all_to_all(send, 'z', split_axis=0, concat_axis=0, tiled=True)  18.1 us
    all_to_all x1, blocking collectives, body(): lax.all_to_all(send, ('y', 'x'), split_axis=0, concat_axis=0, tiled=True)  16.6 us
    all_to_all x1, starting transfers between devices, body(): lax.all_to_all(outgoing.reshape(devices, SLOT_ROWS, width), AXES, split_a...  15.4 us
    all_to_all x1, waiting for transfers between devices, body(): lax.all_to_all(outgoing.reshape(devices, SLOT_ROWS, width), AXES, split_a...  9.15 us
    unnamed x28, local copies, waits for them, and re-layouts  7.22 us
    pallas_call x1, Pallas kernels, interpolate(): pl.pallas_call(interp_kernel, in_specs=[HBM] * 4, out_specs=VMEM, out_sha...  6.91 us
    pallas_call x1, Pallas kernels, outer(): pl.pallas_call(outer_kernel, in_specs=[SMEM] + [VMEM] * 4, out_specs=[VME...  4.22 us
    pallas_call x1, Pallas kernels, inner(): pl.pallas_call(inner_kernel, in_specs=[SMEM, VMEM], out_specs=[VMEM] * 2,...  2.37 us
  transfers between devices with their start and end apart: 2, of which 2 were waited for; matrix products, arithmetic and copies ran while one was open for 0% of the time, Pallas kernels for 3%

profile of v2, /device:TPU:2, one launch (start us, length us, event | category | flops | bytes accessed | tf_op | source)
XLA Modules:
  0.0 87.4 jit_solution(1593309378732916562)
XLA Ops:
  0.6 0.0 copy-start.5
  0.6 0.0 copy-start.4
  0.7 6.9 %shard_map.131 = bf16[64,32,128]{2,1,0:T(8,128)(2,1)} custom-call(bf16[3,1024,128]{2,1,0:T(8,128)(2,1)} %modes_hbm.1, s32[4,1536]{1,0:T(4,128)} %index_hbm.1, f32[4,1536]{1,0:T(4,128)} %interp_hbm.1, f32[3,1536]{1,0:T(4,128)} %normals_hbm.1), custom_call_target="tpu_custom_call" | custom-call | flops 1207959552 | bytes 1048576 | tf_op jit(solution)/shard_map/pallas_call | solution.py:91
  7.6 15.4 %all-to-all-start = ((bf16[128,16,128]{2,1,0:T(8,128)(2,1)}), bf16[128,16,128]{2,1,0:T(8,128)(2,1)S(1)}, u32[]{:S(2)}, u32[]{:S(2)}) async-start(bf16[128,16,128]{2,1,0:T(8,128)(2,1)} %bitcast.21), calls=%async_computation | async-start | bytes 1048576 | tf_op jit(solution)/shard_map/all_to_all | solution.py:454
  23.7 0.1 pad_add_fusion.place_ref
  23.8 0.0 copy-start.6
  23.8 0.5 copy-done.6
  24.3 0.0 copy-done.5
  24.3 0.0 copy-done.4
  24.3 1.6 %copy-done = bf16[1024,1024]{1,0:T(8,128)(2,1)S(1)} copy-done((bf16[1024,1024]{1,0:T(8,128)(2,1)S(1)}, bf16[1024,1024]{1,0:T(8,128)(2,1)}, u32[]{:S(2)}) %copy-start) | copy-done | bytes 2097176
  25.9 0.8 copy-done.8
  26.7 0.8 copy-done.9
  27.5 0.7 copy-done.10
  28.2 0.7 copy-done.11
  28.9 1.9 %shard_map.132 = (bf16[1024,128]{1,0:T(8,128)(2,1)S(1)}, bf16[64,128]{1,0:T(8,128)(2,1)S(1)}, f32[1,2048]{1,0:T(1,128)S(1)}, bf16[1024,256]{1,0:T(8,128)(2,1)S(1)}, f32[1024,128]{1,0:T(8,128)S(1)}) custom-call(s32[4]{0:T(128)S(1)} %pad_add_fusion.place_ref, s32[1]{0:T(128)S(6)} %copy.14.rank_ref, s32[1,128]{1,0:T(1,128)S(1)} %bitcast.20, ...), custom_call_target="tpu_custom_call" | custom-call | flops 4294967296 | bytes 8388608 | tf_op jit(solution)/shard_map/pallas_call | solution.py:154
  30.8 0.0 copy-start.2
  30.8 0.8 copy-done.2
  31.6 0.6 copy-done.12
  32.2 9.1 %all-to-all-done = bf16[128,16,128]{2,1,0:T(8,128)(2,1)S(1)} async-done(((bf16[128,16,128]{2,1,0:T(8,128)(2,1)}), bf16[128,16,128]{2,1,0:T(8,128)(2,1)S(1)}, u32[]{:S(2)}, u32[]{:S(2)}) %all-to-all-start) | async-done | bytes 524320 | tf_op jit(solution)/shard_map/all_to_all | solution.py:454
  41.3 0.7 copy-done.13
  42.0 1.4 %shard_map.133 = (bf16[1024,128]{1,0:T(8,128)(2,1)S(1)}, bf16[128,1024]{1,0:T(8,128)(2,1)S(1)}) custom-call(bf16[2048,128]{1,0:T(8,128)(2,1)S(1)} %bitcast.12, f32[1,2048]{1,0:T(1,128)S(1)} %copy-done.13), custom_call_target="tpu_custom_call" | custom-call | flops 536870912 | bytes 2097152 | tf_op jit(solution)/shard_map/pallas_call | solution.py:193
  43.5 0.1 collective-permute-start
  43.6 0.0 copy-done.1
  43.6 0.9 %shard_map.134 = (f32[1024,128]{1,0:T(8,128)S(1)}, bf16[64,128]{1,0:T(8,128)(2,1)S(1)}) custom-call(bf16[1024,128]{1,0:T(8,128)(2,1)S(1)} %get-tuple-element.14.normal_ref, bf16[1024,1024]{1,0:T(8,128)(2,1)S(1)} %copy-done.1, bf16[32,1024]{1,0:T(8,128)(2,1)S(1)} %bitcast.14, bf16[32,1024]{1,0:T(8,128)(2,1)S(1)} %bitcast.16), custom_call_target="tpu_custom_call" | custom-call | flops 536870912 | bytes 4194304 | tf_op jit(solution)/shard_map/pallas_call | solution.py:220
  44.5 0.6 collective-permute-done.other_ref
  45.1 0.0 copy-done.3
  45.1 0.0 copy-done.7
  45.1 1.0 %shard_map.135 = bf16[8,192,128]{2,1,0:T(8,128)(2,1)S(1)} custom-call(s32[4]{0:T(128)S(1)} %copy-done.7, f32[1024,128]{1,0:T(8,128)S(1)} %get-tuple-element.15.solved_ref, bf16[1024,256]{1,0:T(8,128)(2,1)S(1)} %get-tuple-element.16.scaled_ref, f32[1024,128]{1,0:T(8,128)S(1)} %copy-done.3, bf16[128,1024]{1,0:T(8,128)(2,1)S(1)} %get-tuple-element.18.turned_ref, ...), custom_call_target="tpu_custom_call" | custom-call | flops 268435456 | bytes 2097152 | tf_op jit(solution)/shard_map/pallas_call | solution.py:267
  46.1 18.1 %all_to_all.15.got_ref = bf16[8,192,128]{2,1,0:T(8,128)(2,1)S(1)} all-to-all(bf16[8,192,128]{2,1,0:T(8,128)(2,1)S(1)} %shard_map.135), channel_id=1, replica_groups=mesh['side'=2,'y'=4,'x'=4,'z'=8] {'z'}, dimensions={0} | all-to-all | bytes 786432 | tf_op jit(solution)/shard_map/all_to_all | solution.py:466
  64.2 2.4 %shard_map.136 = (f32[64,256]{1,0:T(8,128)S(1)}, bf16[16,144,128]{2,1,0:T(8,128)(2,1)S(1)}) custom-call(s32[4]{0:T(128)S(1)} %copy-done.7, bf16[8,192,128]{2,1,0:T(8,128)(2,1)S(1)} %all_to_all.15.got_ref), custom_call_target="tpu_custom_call" | custom-call | tf_op jit(solution)/shard_map/pallas_call | solution.py:374
  66.6 16.6 %all_to_all.16.got_ref = bf16[16,144,128]{2,1,0:T(8,128)(2,1)S(1)} all-to-all(bf16[16,144,128]{2,1,0:T(8,128)(2,1)S(1)} %get-tuple-element.21), channel_id=1, replica_groups=mesh['side'=2,'y'=4,'x'=4,'z'=8] {'y','x'}, dimensions={0} | all-to-all | bytes 1179648 | tf_op jit(solution)/shard_map/all_to_all | solution.py:468
  83.2 4.2 %shard_map.137 = (bf16[1024,128]{1,0:T(8,128)(2,1)}, f32[2,128]{1,0:T(2,128)}) custom-call(s32[4]{0:T(128)S(1)} %copy-done.7, bf16[16,144,128]{2,1,0:T(8,128)(2,1)S(1)} %all_to_all.16.got_ref, f32[64,256]{1,0:T(8,128)S(1)} %get-tuple-element.22.own_ref, f32[1024,128]{1,0:T(8,128)S(1)} %get-tuple-element.15.solved_ref, ...), custom_call_target="tpu_custom_call" | custom-call | tf_op jit(solution)/shard_map/pallas_call | solution.py:433
  (10 shorter events, 0.0 us)
Async XLA Ops:
  0.6 23.6 %copy-start.5 = (bf16[1024,32]{0,1:T(8,128)(2,1)S(1)}, bf16[1024,32]{0,1:T(8,128)(2,1)}, u32[]{:S(2)}) copy-start(bf16[1024,32]{0,1:T(8,128)(2,1)} %param.21) | copy-start | bytes 196612
  0.6 23.6 %copy-start.4 = (bf16[1024,32]{0,1:T(8,128)(2,1)S(1)}, bf16[1024,32]{0,1:T(8,128)(2,1)}, u32[]{:S(2)}) copy-start(bf16[1024,32]{0,1:T(8,128)(2,1)} %param.19) | copy-start | bytes 196612
  7.6 33.8 %all-to-all-start = ((bf16[128,16,128]{2,1,0:T(8,128)(2,1)}), bf16[128,16,128]{2,1,0:T(8,128)(2,1)S(1)}, u32[]{:S(2)}, u32[]{:S(2)}) async-start(bf16[128,16,128]{2,1,0:T(8,128)(2,1)} %bitcast.21), calls=%async_computation | async-start | bytes 1048576 | tf_op jit(solution)/shard_map/all_to_all | solution.py:454
  23.8 0.5 copy-start.6
  24.3 1.6 %copy-start = (bf16[1024,1024]{1,0:T(8,128)(2,1)S(1)}, bf16[1024,1024]{1,0:T(8,128)(2,1)}, u32[]{:S(2)}) copy-start(bf16[1024,1024]{1,0:T(8,128)(2,1)} %diag_ref.3) | copy-start | bytes 6291460
  25.9 0.8 copy-start.8
  26.7 0.8 copy-start.9
  27.5 0.7 copy-start.10
  28.2 0.7 copy-start.11
  28.9 14.7 %copy-start.1 = (bf16[1024,1024]{1,0:T(8,128)(2,1)S(1)}, bf16[1024,1024]{1,0:T(8,128)(2,1)}, u32[]{:S(2)}) copy-start(bf16[1024,1024]{1,0:T(8,128)(2,1)} %diag_ref.3) | copy-start | bytes 6291460
  30.8 0.8 copy-start.2
  31.6 0.6 copy-start.12
  41.3 0.7 copy-start.13
  42.0 3.0 %copy-start.3 = (f32[1024,128]{1,0:T(8,128)S(1)}, f32[1024,128]{1,0:T(8,128)}, u32[]{:S(2)}) copy-start(f32[1024,128]{1,0:T(8,128)} %copy-done.2) | copy-start | bytes 1572868
  42.0 3.0 %copy-start.7 = (s32[4]{0:T(128)S(1)}, s32[4]{0:T(128)}, u32[]{:S(2)}) copy-start(s32[4]{0:T(128)} %copy-done.6) | copy-start | bytes 52
  43.5 1.6 %collective-permute-start = (bf16[128,1024]{1,0:T(8,128)(2,1)S(1)}, bf16[128,1024]{1,0:T(8,128)(2,1)S(1)}, u32[]{:S(2)}, u32[]{:S(2)}) collective-permute-start(bf16[128,1024]{1,0:T(8,128)(2,1)S(1)} %get-tuple-element.18.turned_ref), channel_id=1, source_target_pairs={{0,128},{128,0},{1,129},{129,1},{2,130},{130,2},{3,131},{131,3},{4... | collective-permute-start | bytes 786440 | tf_op jit(solution)/shard_map/ppermute | solution.py:463

commit v3 on v2

--- a/solution.py
+++ b/solution.py
@@ -14,7 +14,7 @@
 VMEM = pl.BlockSpec(memory_space=pltpu.VMEM)
 SMEM = pl.BlockSpec(memory_space=pltpu.SMEM)
 HBM = pl.BlockSpec(memory_space=pltpu.HBM)
-STEPS, TURN = 4, 128
+STEPS, TURN, GROUPS = 4, 128, 4
 
 
 def mm(a, b):
@@ -171,15 +171,18 @@
 
 def select_kernel(arrived_ref, target_ref, normal_ref, turned_ref):
     panels, width = normal_ref.shape
-    slots = target_ref.shape[1]
+    target = target_ref[...]
+    sources = target.shape[1] // SLOT_ROWS
     step = 256
-    target = target_ref[...]
-    arrived = arrived_ref[...]
     parts = []
     for begin in range(0, panels, step):
-        panel = (lax.broadcasted_iota(I32, (step, slots), 0) + begin).astype(F32)
-        pick = jnp.where(panel == target, 1.0, 0.0).astype(BF16)
-        parts.append(mm(pick, arrived).astype(BF16))
+        least = max(0, (begin - CAP + 1) // CAP)
+        most = min(sources, (begin + step - 1 + CAP * sources - panels) // CAP + 1)
+        first = least * SLOT_ROWS // 128 * 128
+        last = -(-most * SLOT_ROWS // 128) * 128
+        panel = (lax.broadcasted_iota(I32, (step, last - first), 0) + begin).astype(F32)
+        pick = jnp.where(panel == target[:, first:last], 1.0, 0.0).astype(BF16)
+        parts.append(mm(pick, arrived_ref[first:last, :]).astype(BF16))
     normal = jnp.concatenate(parts, axis=0)
     normal_ref[...] = normal
     row = lax.broadcasted_iota(I32, (width, width), 0)
@@ -250,11 +253,9 @@
     mats = mats_ref[...].astype(F32)
     for side in range(2):
         rows = jnp.where(even, other, own) if side else jnp.where(even, own, other)
-        high, low = halves(rows[:, :width])
         begin = 4 * RANK + side * part
-        send_ref[:, begin : begin + part, :] = high.reshape(peers, part, width)
-        begin = begin + RANK
-        send_ref[:, begin : begin + part, :] = low.reshape(peers, part, width)
+        fixed = rows[:, :width].astype(BF16)
+        send_ref[:, begin : begin + part, :] = fixed.reshape(peers, part, width)
         for which in range(2):
             begin = which * RANK + side * part
             block = rows[:, (1 + which) * width : (2 + which) * width].reshape(peers, part, width)
@@ -268,7 +269,7 @@
         local_kernel,
         in_specs=[SMEM] + [VMEM] * 7,
         out_specs=VMEM,
-        out_shape=jax.ShapeDtypeStruct((peers, 6 * RANK, width), BF16),
+        out_shape=jax.ShapeDtypeStruct((peers, 5 * RANK, width), BF16),
         compiler_params=PARAMS,
         cost_estimate=pl.CostEstimate(
             flops=1 << 28, bytes_accessed=2 << 20, transcendentals=0
@@ -306,39 +307,51 @@
     return jnp.where(lane == row + offset, 1.0, 0.0).astype(F32)
 
 
+def advance(forward, total, parts, mask):
+    shift, gain, ahead, back, by_s, by_t, fixed = parts
+    width = fixed.shape[1]
+    pad = jnp.zeros((RANK, WIDE - width), F32)
+    gap, tail = jnp.zeros((RANK, width), F32), jnp.zeros((RANK, WIDE - width - RANK), F32)
+    moved = mm(jnp.concatenate(ahead + [by_s], axis=0), tall(forward))
+    later = forward + moved[:RANK] + jnp.concatenate([shift, pad], axis=1)
+    middle = (
+        jnp.concatenate([gain, pad], axis=1)
+        + jnp.concatenate([gap, back, tail], axis=1)
+        - moved[RANK : 2 * RANK]
+    )
+    mass = moved[2 * RANK :] + jnp.concatenate([fixed, by_t, tail[: fixed.shape[0]]], axis=1)
+    none = jnp.zeros((2 * RANK, WIDE), F32)
+    total = gain_step(total, mask, middle) + jnp.concatenate([none, mass], axis=0)
+    return later, total
+
+
+def own_mask(rows, keep):
+    row = lax.broadcasted_iota(I32, (rows, RANK), 0)
+    return jnp.where((row >= RANK) & (row < 2 * RANK) & jnp.logical_not(keep), 0.0, 1.0)
+
+
+def start_total(rows):
+    head = [unit(TURN), unit(TURN)]
+    return jnp.concatenate(head + [jnp.zeros((rows, WIDE), F32)], axis=0)
+
+
 def inner_kernel(place_ref, got_ref, own_ref, send_ref):
     width = got_ref.shape[2]
     mine = place_ref[0]
     in_t, in_s = TURN, TURN + RANK
-    forward = unit(in_s)
+    forward, total = unit(in_s), start_total(RANK)
     own_s = jnp.zeros_like(forward)
-    total = jnp.concatenate([unit(in_t), unit(in_t), jnp.zeros((RANK, WIDE), F32)], axis=0)
-    pad = jnp.zeros((RANK, WIDE - width), F32)
-    gap, tail = jnp.zeros((RANK, width), F32), jnp.zeros((RANK, WIDE - width - RANK), F32)
-    none = jnp.zeros((2 * RANK, WIDE), F32)
     blank = jnp.zeros((RANK, RANK), BF16)
-    row = lax.broadcasted_iota(I32, (3 * RANK, RANK), 0)
-    middle_rows = (row >= RANK) & (row < 2 * RANK)
     for position in range(got_ref.shape[0]):
-        shift, gain, ahead, back = element(got_ref, position)
         by_s = got_ref[position, 2 * RANK : 3 * RANK, 3 * RANK : 4 * RANK]
         by_t = got_ref[position, 3 * RANK : 4 * RANK, 3 * RANK : 4 * RANK].astype(F32)
         fixed = got_ref[position, 4 * RANK : 5 * RANK, :].astype(F32)
-        fixed = fixed + got_ref[position, 5 * RANK : 6 * RANK, :].astype(F32)
-        ahead = jnp.concatenate(
-            ahead + [jnp.concatenate([by_s, blank, by_s], axis=1)], axis=0
+        by_s = jnp.concatenate([by_s, blank, by_s], axis=1)
+        own_s = jnp.where(mine == position, forward, own_s)
+        forward, total = advance(
+            forward, total, element(got_ref, position) + (by_s, by_t, fixed),
+            own_mask(3 * RANK, position > mine),
         )
-        own_s = jnp.where(mine == position, forward, own_s)
-        moved = mm(ahead, tall(forward))
-        forward = forward + moved[:RANK] + jnp.concatenate([shift, pad], axis=1)
-        middle = (
-            jnp.concatenate([gain, pad], axis=1)
-            + jnp.concatenate([gap, back, tail], axis=1)
-            - moved[RANK : 2 * RANK]
-        )
-        mask = jnp.where(middle_rows & (position <= mine), 0.0, 1.0)
-        mass = moved[2 * RANK :] + jnp.concatenate([fixed, by_t, tail], axis=1)
-        total = gain_step(total, mask, middle) + jnp.concatenate([none, mass], axis=0)
     own_ref[...] = jnp.concatenate([own_s, total[RANK : 2 * RANK]], axis=0)
     eye = unit(0)[:, :RANK]
     mats = jnp.concatenate(
@@ -387,38 +400,81 @@
     place_ref, got_ref, own_ref, solved_ref, stack_ref, potential_ref, mass_ref,
 ):
     width = got_ref.shape[2]
-    mine = place_ref[1]
-    forward = jnp.zeros((RANK, width), F32)
-    in_s = forward
-    total = jnp.concatenate([unit(TURN), jnp.zeros((16, WIDE), F32)], axis=0)
-    rest = jnp.zeros((RANK, WIDE - width - RANK), F32)
-    none, low_rest = jnp.zeros((RANK, WIDE), F32), jnp.zeros((16, WIDE - width - RANK), F32)
-    zero8, zero16 = jnp.zeros((8, 4 * RANK), F32), jnp.zeros((16, RANK), BF16)
-    row = lax.broadcasted_iota(I32, (RANK + 16, RANK), 0)
-    for position in range(got_ref.shape[0]):
-        shift, gain, ahead, back = element(got_ref, position)
-        fixed = got_ref[position, 4 * RANK :, :].astype(F32)
-        maps = jnp.concatenate([fixed[8:16], zero8], axis=0)
-        by_s_high = maps[:, :RANK].astype(BF16)
-        by_s_low = maps[:, RANK : 2 * RANK].astype(BF16)
-        by_t = maps[:, 2 * RANK : 3 * RANK] + maps[:, 3 * RANK :]
-        ahead = jnp.concatenate(
-            ahead + [jnp.concatenate([by_s_high, by_s_low, by_s_high], axis=1)], axis=0
-        )
-        in_s = jnp.where(mine == position, forward, in_s)
-        moved = mm(ahead, tall(forward))
-        forward = forward + moved[:RANK] + shift
-        middle = jnp.concatenate([gain - moved[RANK : 2 * RANK], back, rest], axis=1)
-        mask = jnp.where((row < RANK) & (position <= mine), 0.0, 1.0)
-        mass = jnp.concatenate([fixed + moved[2 * RANK :], by_t, low_rest], axis=1)
-        total = gain_step(total, mask, middle) + jnp.concatenate([none, mass], axis=0)
-    in_t = total[:RANK, :width]
-    mass = total[RANK:, :width]
-    mass_ref[...] = mass[0:2] + mass[2:4]
+    groups = GROUPS
+    members = got_ref.shape[0] // groups
+    my_group, my_member = place_ref[1] // members, place_ref[1] % members
+    in_t, in_s = TURN, TURN + RANK
+    forwards = [unit(in_s)] * groups
+    totals = [start_total(16)] * groups
+    own_s = jnp.zeros((RANK, WIDE), F32)
+    zero8 = jnp.zeros((8, 4 * RANK), F32)
+    for member in range(members):
+        mask = own_mask(2 * RANK + 16, member > my_member)
+        for group in range(groups):
+            position = group * members + member
+            fixed = got_ref[position, 4 * RANK :, :].astype(F32)
+            maps = jnp.concatenate([fixed[8:16], zero8], axis=0)
+            by_s = maps[:, :RANK].astype(BF16)
+            by_s = jnp.concatenate(
+                [by_s, maps[:, RANK : 2 * RANK].astype(BF16), by_s], axis=1
+            )
+            by_t = maps[:, 2 * RANK : 3 * RANK] + maps[:, 3 * RANK :]
+            here = (my_group == group) & (my_member == member)
+            own_s = jnp.where(here, forwards[group], own_s)
+            forwards[group], totals[group] = advance(
+                forwards[group], totals[group],
+                element(got_ref, position) + (by_s, by_t, fixed), mask,
+            )
+    own_t = jnp.zeros((RANK, WIDE), F32)
+    for group in range(groups):
+        own_t = jnp.where(my_group == group, totals[group][RANK : 2 * RANK], own_t)
     own = own_ref[...]
     map_high, map_low = halves(own[:, width : width + 2 * RANK])
     maps = jnp.concatenate([map_high, map_low, map_high], axis=1)
-    state = own[:, :width] + mm(maps, tall(jnp.concatenate([in_t, in_s], axis=0)))
+    lanes = lax.broadcasted_iota(I32, own.shape, 1)
+    own = jnp.where(lanes < width, own, 0.0) + mm(
+        maps, tall(jnp.concatenate([own_t, own_s], axis=0))
+    )
+    eye = unit(0)[:, :RANK]
+    forward = jnp.zeros((RANK, width), F32)
+    enter_s = forward
+    total = jnp.concatenate([unit(TURN), jnp.zeros((16, WIDE), F32)], axis=0)
+    none, rest = jnp.zeros((RANK, WIDE), F32), jnp.zeros((RANK, WIDE - width - RANK), F32)
+    row = lax.broadcasted_iota(I32, (RANK + 16, RANK), 0)
+    for group in range(groups):
+        step, whole = forwards[group], totals[group]
+        mass = whole[2 * RANK :]
+        ahead = jnp.concatenate(
+            [
+                step[:, in_s : in_s + RANK] - eye,
+                whole[:RANK, in_s : in_s + RANK],
+                mass[:, in_s : in_s + RANK],
+            ],
+            axis=0,
+        )
+        high, low = halves(ahead)
+        enter_s = jnp.where(my_group == group, forward, enter_s)
+        moved = mm(jnp.concatenate([high, low, high], axis=1), tall(forward))
+        forward = forward + moved[:RANK] + step[:, :width]
+        middle = jnp.concatenate(
+            [
+                whole[:RANK, :width] + moved[RANK : 2 * RANK],
+                whole[:RANK, in_t : in_t + RANK] - eye,
+                rest,
+            ],
+            axis=1,
+        )
+        mask = jnp.where((row < RANK) & (group <= my_group), 0.0, 1.0)
+        mass = jnp.concatenate(
+            [mass[:, :width] + moved[2 * RANK :], mass[:, in_t : in_t + RANK], rest[:16]], axis=1
+        )
+        total = gain_step(total, mask, middle) + jnp.concatenate([none, mass], axis=0)
+    enter_t = total[:RANK, :width]
+    mass = total[RANK:, :width]
+    mass_ref[...] = mass[0:2] + mass[2:4]
+    map_high, map_low = halves(own[:, width : width + 2 * RANK])
+    maps = jnp.concatenate([map_high, map_low, map_high], axis=1)
+    state = own[:, :width] + mm(maps, tall(jnp.concatenate([enter_t, enter_s], axis=0)))
     high, low = halves(state)
     blank = jnp.zeros((RANK, width), BF16)
     left = jnp.concatenate([high, high[:RANK], blank], axis=0)

time: 88.6 us -> 85.9 us (0.970)
  blocking collectives: 34.7 us -> 32.7 us
    all_to_all x1, blocking collectives: 18.1 us -> 16.7 us  [body(): got = lax.all_to_all(send, 'z', split_axis=0, concat_axis=0, tiled=True)]
where the time goes in v3:
time: 85.9 us; the launch traced here: 85 us
  blocking collectives  32.7 us (38%)
  Pallas kernels  18.3 us (21%)
  starting transfers between devices  15.5 us (18%)
  waiting for transfers between devices  9.74 us (11%)
  local copies, waits for them, and re-layouts  7.22 us (8%)
  between operations  1.4 us (2%)
    all_to_all x1, blocking collectives, body(): got = lax.all_to_all(send, 'z', split_axis=0, concat_axis=0, tiled=True)  16.7 us
    all_to_all x1, blocking collectives, body(): lax.all_to_all(send, ('y', 'x'), split_axis=0, concat_axis=0, tiled=True)  16 us
    all_to_all x1, starting transfers between devices, body(): lax.all_to_all(outgoing.reshape(devices, SLOT_ROWS, width), AXES, split_a...  15.4 us
    all_to_all x1, waiting for transfers between devices, body(): lax.all_to_all(outgoing.reshape(devices, SLOT_ROWS, width), AXES, split_a...  9.15 us
    unnamed x28, local copies, waits for them, and re-layouts  7.22 us
    pallas_call x1, Pallas kernels, interpolate(): pl.pallas_call(interp_kernel, in_specs=[HBM] * 4, out_specs=VMEM, out_sha...  6.91 us
    pallas_call x1, Pallas kernels, outer(): pl.pallas_call(outer_kernel, in_specs=[SMEM] + [VMEM] * 4, out_specs=[VME...  4.3 us
    pallas_call x1, Pallas kernels, inner(): pl.pallas_call(inner_kernel, in_specs=[SMEM, VMEM], out_specs=[VMEM] * 2,...  2.37 us
  transfers between devices with their start and end apart: 2, of which 2 were waited for; matrix products, arithmetic and copies ran while one was open for 0% of the time, Pallas kernels for 3%

profile of v3, /device:TPU:2, one launch (start us, length us, event | category | flops | bytes accessed | tf_op | source)
XLA Modules:
  0.0 85.0 jit_solution(332425901660372125)
XLA Ops:
  0.6 0.0 copy-start.5
  0.6 0.0 copy-start.4
  0.7 6.9 %shard_map.131 = bf16[64,32,128]{2,1,0:T(8,128)(2,1)} custom-call(bf16[3,1024,128]{2,1,0:T(8,128)(2,1)} %modes_hbm.1, s32[4,1536]{1,0:T(4,128)} %index_hbm.1, f32[4,1536]{1,0:T(4,128)} %interp_hbm.1, f32[3,1536]{1,0:T(4,128)} %normals_hbm.1), custom_call_target="tpu_custom_call" | custom-call | flops 1207959552 | bytes 1048576 | tf_op jit(solution)/shard_map/pallas_call | solution.py:91
  7.6 15.4 %all-to-all-start = ((bf16[128,16,128]{2,1,0:T(8,128)(2,1)}), bf16[128,16,128]{2,1,0:T(8,128)(2,1)S(1)}, u32[]{:S(2)}, u32[]{:S(2)}) async-start(bf16[128,16,128]{2,1,0:T(8,128)(2,1)} %bitcast.21), calls=%async_computation | async-start | bytes 1048576 | tf_op jit(solution)/shard_map/all_to_all | solution.py:510
  23.7 0.1 pad_add_fusion.place_ref
  23.8 0.0 copy-start.6
  23.8 0.5 copy-done.6
  24.3 0.0 copy-done.5
  24.3 0.0 copy-done.4
  24.3 1.6 %copy-done = bf16[1024,1024]{1,0:T(8,128)(2,1)S(1)} copy-done((bf16[1024,1024]{1,0:T(8,128)(2,1)S(1)}, bf16[1024,1024]{1,0:T(8,128)(2,1)}, u32[]{:S(2)}) %copy-start) | copy-done | bytes 2097176
  25.9 0.8 copy-done.8
  26.7 0.8 copy-done.9
  27.5 0.7 copy-done.10
  28.2 0.7 copy-done.11
  28.9 1.9 %shard_map.132 = (bf16[1024,128]{1,0:T(8,128)(2,1)S(1)}, bf16[64,128]{1,0:T(8,128)(2,1)S(1)}, f32[1,2048]{1,0:T(1,128)S(1)}, bf16[1024,256]{1,0:T(8,128)(2,1)S(1)}, f32[1024,128]{1,0:T(8,128)S(1)}) custom-call(s32[4]{0:T(128)S(1)} %pad_add_fusion.place_ref, s32[1]{0:T(128)S(6)} %copy.14.rank_ref, s32[1,128]{1,0:T(1,128)S(1)} %bitcast.20, ...), custom_call_target="tpu_custom_call" | custom-call | flops 4294967296 | bytes 8388608 | tf_op jit(solution)/shard_map/pallas_call | solution.py:154
  30.8 0.0 copy-start.2
  30.8 0.8 copy-done.2
  31.6 0.6 copy-done.12
  32.2 9.1 %all-to-all-done = bf16[128,16,128]{2,1,0:T(8,128)(2,1)S(1)} async-done(((bf16[128,16,128]{2,1,0:T(8,128)(2,1)}), bf16[128,16,128]{2,1,0:T(8,128)(2,1)S(1)}, u32[]{:S(2)}, u32[]{:S(2)}) %all-to-all-start) | async-done | bytes 524320 | tf_op jit(solution)/shard_map/all_to_all | solution.py:510
  41.3 0.7 copy-done.13
  42.0 0.9 %shard_map.133 = (bf16[1024,128]{1,0:T(8,128)(2,1)S(1)}, bf16[128,1024]{1,0:T(8,128)(2,1)S(1)}) custom-call(bf16[2048,128]{1,0:T(8,128)(2,1)S(1)} %bitcast.12, f32[1,2048]{1,0:T(1,128)S(1)} %copy-done.13), custom_call_target="tpu_custom_call" | custom-call | flops 536870912 | bytes 2097152 | tf_op jit(solution)/shard_map/pallas_call | solution.py:196
  43.0 0.1 collective-permute-start
  43.1 0.0 copy-done.1
  43.1 0.9 %shard_map.134 = (f32[1024,128]{1,0:T(8,128)S(1)}, bf16[64,128]{1,0:T(8,128)(2,1)S(1)}) custom-call(bf16[1024,128]{1,0:T(8,128)(2,1)S(1)} %get-tuple-element.14.normal_ref, bf16[1024,1024]{1,0:T(8,128)(2,1)S(1)} %copy-done.1, bf16[32,1024]{1,0:T(8,128)(2,1)S(1)} %bitcast.14, bf16[32,1024]{1,0:T(8,128)(2,1)S(1)} %bitcast.16), custom_call_target="tpu_custom_call" | custom-call | flops 536870912 | bytes 4194304 | tf_op jit(solution)/shard_map/pallas_call | solution.py:223
  44.0 0.6 collective-permute-done.other_ref
  44.6 0.0 copy-done.3
  44.6 0.0 copy-done.7
  44.6 1.0 %shard_map.135 = bf16[8,160,128]{2,1,0:T(8,128)(2,1)S(1)} custom-call(s32[4]{0:T(128)S(1)} %copy-done.7, f32[1024,128]{1,0:T(8,128)S(1)} %get-tuple-element.15.solved_ref, bf16[1024,256]{1,0:T(8,128)(2,1)S(1)} %get-tuple-element.16.scaled_ref, f32[1024,128]{1,0:T(8,128)S(1)} %copy-done.3, bf16[128,1024]{1,0:T(8,128)(2,1)S(1)} %get-tuple-element.18.turned_ref, ...), custom_call_target="tpu_custom_call" | custom-call | flops 268435456 | bytes 2097152 | tf_op jit(solution)/shard_map/pallas_call | solution.py:268
  45.6 16.7 %all_to_all.15.got_ref = bf16[8,160,128]{2,1,0:T(8,128)(2,1)S(1)} all-to-all(bf16[8,160,128]{2,1,0:T(8,128)(2,1)S(1)} %shard_map.135), channel_id=1, replica_groups=mesh['side'=2,'y'=4,'x'=4,'z'=8] {'z'}, dimensions={0} | all-to-all | bytes 655360 | tf_op jit(solution)/shard_map/all_to_all | solution.py:522
  62.3 2.4 %shard_map.136 = (f32[64,256]{1,0:T(8,128)S(1)}, bf16[16,144,128]{2,1,0:T(8,128)(2,1)S(1)}) custom-call(s32[4]{0:T(128)S(1)} %copy-done.7, bf16[8,160,128]{2,1,0:T(8,128)(2,1)S(1)} %all_to_all.15.got_ref), custom_call_target="tpu_custom_call" | custom-call | tf_op jit(solution)/shard_map/pallas_call | solution.py:387
  64.7 16.0 %all_to_all.16.got_ref = bf16[16,144,128]{2,1,0:T(8,128)(2,1)S(1)} all-to-all(bf16[16,144,128]{2,1,0:T(8,128)(2,1)S(1)} %get-tuple-element.21), channel_id=1, replica_groups=mesh['side'=2,'y'=4,'x'=4,'z'=8] {'y','x'}, dimensions={0} | all-to-all | bytes 1179648 | tf_op jit(solution)/shard_map/all_to_all | solution.py:524
  80.7 4.3 %shard_map.137 = (bf16[1024,128]{1,0:T(8,128)(2,1)}, f32[2,128]{1,0:T(2,128)}) custom-call(s32[4]{0:T(128)S(1)} %copy-done.7, bf16[16,144,128]{2,1,0:T(8,128)(2,1)S(1)} %all_to_all.16.got_ref, f32[64,256]{1,0:T(8,128)S(1)} %get-tuple-element.22.own_ref, f32[1024,128]{1,0:T(8,128)S(1)} %get-tuple-element.15.solved_ref, ...), custom_call_target="tpu_custom_call" | custom-call | tf_op jit(solution)/shard_map/pallas_call | solution.py:489
  (10 shorter events, 0.0 us)
Async XLA Ops:
  0.6 23.6 %copy-start.5 = (bf16[1024,32]{0,1:T(8,128)(2,1)S(1)}, bf16[1024,32]{0,1:T(8,128)(2,1)}, u32[]{:S(2)}) copy-start(bf16[1024,32]{0,1:T(8,128)(2,1)} %param.21) | copy-start | bytes 196612
  0.6 23.6 %copy-start.4 = (bf16[1024,32]{0,1:T(8,128)(2,1)S(1)}, bf16[1024,32]{0,1:T(8,128)(2,1)}, u32[]{:S(2)}) copy-start(bf16[1024,32]{0,1:T(8,128)(2,1)} %param.19) | copy-start | bytes 196612
  7.6 33.8 %all-to-all-start = ((bf16[128,16,128]{2,1,0:T(8,128)(2,1)}), bf16[128,16,128]{2,1,0:T(8,128)(2,1)S(1)}, u32[]{:S(2)}, u32[]{:S(2)}) async-start(bf16[128,16,128]{2,1,0:T(8,128)(2,1)} %bitcast.21), calls=%async_computation | async-start | bytes 1048576 | tf_op jit(solution)/shard_map/all_to_all | solution.py:510
  23.8 0.5 copy-start.6
  24.3 1.6 %copy-start = (bf16[1024,1024]{1,0:T(8,128)(2,1)S(1)}, bf16[1024,1024]{1,0:T(8,128)(2,1)}, u32[]{:S(2)}) copy-start(bf16[1024,1024]{1,0:T(8,128)(2,1)} %diag_ref.3) | copy-start | bytes 6291460
  25.9 0.8 copy-start.8
  26.7 0.8 copy-start.9
  27.5 0.7 copy-start.10
  28.2 0.7 copy-start.11
  28.9 14.2 %copy-start.1 = (bf16[1024,1024]{1,0:T(8,128)(2,1)S(1)}, bf16[1024,1024]{1,0:T(8,128)(2,1)}, u32[]{:S(2)}) copy-start(bf16[1024,1024]{1,0:T(8,128)(2,1)} %diag_ref.3) | copy-start | bytes 6291460
  30.8 0.8 copy-start.2
  31.6 0.6 copy-start.12
  41.3 0.7 copy-start.13
  42.0 2.6 %copy-start.3 = (f32[1024,128]{1,0:T(8,128)S(1)}, f32[1024,128]{1,0:T(8,128)}, u32[]{:S(2)}) copy-start(f32[1024,128]{1,0:T(8,128)} %copy-done.2) | copy-start | bytes 1572868
  42.0 2.6 %copy-start.7 = (s32[4]{0:T(128)S(1)}, s32[4]{0:T(128)}, u32[]{:S(2)}) copy-start(s32[4]{0:T(128)} %copy-done.6) | copy-start | bytes 52
  43.0 1.6 %collective-permute-start = (bf16[128,1024]{1,0:T(8,128)(2,1)S(1)}, bf16[128,1024]{1,0:T(8,128)(2,1)S(1)}, u32[]{:S(2)}, u32[]{:S(2)}) collective-permute-start(bf16[128,1024]{1,0:T(8,128)(2,1)S(1)} %get-tuple-element.18.turned_ref), channel_id=1, source_target_pairs={{0,128},{128,0},{1,129},{129,1},{2,130},{130,2},{3,131},{131,3},{4... | collective-permute-start | bytes 786440 | tf_op jit(solution)/shard_map/ppermute | solution.py:519

commit v4 on v3

--- a/solution.py
+++ b/solution.py
@@ -14,7 +14,8 @@
 VMEM = pl.BlockSpec(memory_space=pltpu.VMEM)
 SMEM = pl.BlockSpec(memory_space=pltpu.SMEM)
 HBM = pl.BlockSpec(memory_space=pltpu.HBM)
-STEPS, TURN, GROUPS = 4, 128, 4
+STEPS, TURN, GROUPS = 4, 128, 2
+TILE, LANES, ROWS = 32, 256, 192
 
 
 def mm(a, b):
@@ -36,8 +37,8 @@
 
 
 def interp_kernel(
-    modes_hbm, index_hbm, interp_hbm, normals_hbm, out_ref,
-    modes_ref, index_ref, interp_ref, normals_ref, sems,
+    modes_hbm, index_hbm, interp_hbm, normals_hbm, out_hbm,
+    modes_ref, index_ref, interp_ref, normals_ref, high_ref, low_ref, out_ref, sems, out_sems,
 ):
     pairs = [
         (index_hbm, index_ref), (interp_hbm, interp_ref), (normals_hbm, normals_ref),
@@ -54,7 +55,8 @@
     slots, nodes = index_ref.shape[1], modes_ref.shape[1]
     width = modes_ref.shape[2]
     chunk = slots // STEPS
-    node = lax.broadcasted_iota(I32, (chunk, nodes), 1).astype(F32)
+    node = lax.broadcasted_iota(I32, (TILE, nodes), 1).astype(F32)
+    leaving = []
     for step in range(STEPS):
         lanes = slice(step * chunk, (step + 1) * chunk)
         rows = jnp.concatenate(
@@ -67,23 +69,39 @@
             axis=0,
         )
         columns = rows.T
-        mix = jnp.zeros((chunk, nodes), F32)
-        for corner in range(4):
-            here = columns[:, corner : corner + 1] == node
-            mix = mix + jnp.where(here, columns[:, 4 + corner : 5 + corner], 0.0)
-        high, low = halves(mix)
         if step == 0:
             copies[3].wait()
+        for begin in range(0, chunk, TILE):
+            part = columns[begin : begin + TILE]
+            for lane in range(0, nodes, LANES):
+                mix = jnp.zeros((TILE, LANES), F32)
+                for corner in range(4):
+                    here = part[:, corner : corner + 1] == node[:, lane : lane + LANES]
+                    mix = mix + jnp.where(here, part[:, 4 + corner : 5 + corner], 0.0)
+                high, low = halves(mix)
+                high_ref[step % 2, begin : begin + TILE, lane : lane + LANES] = high
+                low_ref[step % 2, begin : begin + TILE, lane : lane + LANES] = low
         table = jnp.concatenate([modes_ref[0], modes_ref[1], modes_ref[2]], axis=1)
-        picked = mm(high, table) + mm(low, table)
-        velocity = jnp.zeros((chunk, width), F32)
-        for axis_id in range(3):
-            part = picked[:, axis_id * width : (axis_id + 1) * width]
-            velocity = velocity + columns[:, 8 + axis_id : 9 + axis_id] * part
-        blocks = velocity.reshape(chunk // 24, 24, width)
-        where = slice(step * chunk // 24, (step + 1) * chunk // 24)
-        out_ref[where, 0:16, :] = blocks[:, 0:16, :].astype(BF16)
-        out_ref[where, 16:32, :] = blocks[:, 8:24, :].astype(BF16)
+        for begin in range(0, chunk, ROWS):
+            picked = mm(high_ref[step % 2, begin : begin + ROWS], table) + mm(
+                low_ref[step % 2, begin : begin + ROWS], table
+            )
+            velocity = jnp.zeros((ROWS, width), F32)
+            for axis_id in range(3):
+                part = picked[:, axis_id * width : (axis_id + 1) * width]
+                normal = columns[begin : begin + ROWS, 8 + axis_id : 9 + axis_id]
+                velocity = velocity + normal * part
+            blocks = velocity.reshape(ROWS // 24, 24, width)
+            where = slice((step * chunk + begin) // 24, (step * chunk + begin + ROWS) // 24)
+            out_ref[where, 0:16, :] = blocks[:, 0:16, :].astype(BF16)
+            out_ref[where, 16:32, :] = blocks[:, 8:24, :].astype(BF16)
+        where = pl.ds(step * chunk // 24, chunk // 24)
+        leaving.append(
+            pltpu.make_async_copy(out_ref.at[where], out_hbm.at[where], out_sems.at[step])
+        )
+        leaving[-1].start()
+    for copy in leaving:
+        copy.wait()
 
 
 def interpolate(node_modes, node_index, interp, normals):
@@ -91,14 +109,18 @@
     return pl.pallas_call(
         interp_kernel,
         in_specs=[HBM] * 4,
-        out_specs=VMEM,
+        out_specs=HBM,
         out_shape=jax.ShapeDtypeStruct((slots // 24, 32, width), BF16),
         scratch_shapes=[
             pltpu.VMEM(node_modes.shape, BF16),
             pltpu.VMEM(node_index.shape, I32),
             pltpu.VMEM(interp.shape, F32),
             pltpu.VMEM(normals.shape, F32),
+            pltpu.VMEM((2, slots // STEPS, node_modes.shape[1]), BF16),
+            pltpu.VMEM((2, slots // STEPS, node_modes.shape[1]), BF16),
+            pltpu.VMEM((slots // 24, 32, width), BF16),
             pltpu.SemaphoreType.DMA((4,)),
+            pltpu.SemaphoreType.DMA((STEPS,)),
         ],
         compiler_params=WHOLE,
         cost_estimate=pl.CostEstimate(

time: 85.9 us -> 85.5 us (level)
  no operation moved by 1% of the time
where the time goes in v4:
time: 85.5 us; the launch traced here: 84.6 us
  blocking collectives  32.7 us (38%)
  Pallas kernels  17.8 us (21%)
  starting transfers between devices  15.5 us (18%)
  waiting for transfers between devices  9.75 us (11%)
  local copies, waits for them, and re-layouts  7.22 us (8%)
  between operations  1.4 us (2%)
    all_to_all x1, blocking collectives, body(): got = lax.all_to_all(send, 'z', split_axis=0, concat_axis=0, tiled=True)  16.7 us
    all_to_all x1, blocking collectives, body(): lax.all_to_all(send, ('y', 'x'), split_axis=0, concat_axis=0, tiled=True)  16 us
    all_to_all x1, starting transfers between devices, body(): lax.all_to_all(outgoing.reshape(devices, SLOT_ROWS, width), AXES, split_a...  15.4 us
    all_to_all x1, waiting for transfers between devices, body(): lax.all_to_all(outgoing.reshape(devices, SLOT_ROWS, width), AXES, split_a...  9.17 us
    unnamed x28, local copies, waits for them, and re-layouts  7.22 us
    pallas_call x1, Pallas kernels, interpolate(): pl.pallas_call(interp_kernel, in_specs=[HBM] * 4, out_specs=HBM, out_shap...  6.71 us
    pallas_call x1, Pallas kernels, outer(): pl.pallas_call(outer_kernel, in_specs=[SMEM] + [VMEM] * 4, out_specs=[VME...  4.03 us
    pallas_call x1, Pallas kernels, inner(): pl.pallas_call(inner_kernel, in_specs=[SMEM, VMEM], out_specs=[VMEM] * 2,...  2.37 us
  transfers between devices with their start and end apart: 2, of which 2 were waited for; matrix products, arithmetic and copies ran while one was open for 0% of the time, Pallas kernels for 3%

profile of v4, /device:TPU:2, one launch (start us, length us, event | category | flops | bytes accessed | tf_op | source)
XLA Modules:
  0.0 84.6 jit_solution(242668411540151515)
XLA Ops:
  0.6 0.0 copy-start.5
  0.6 0.0 copy-start.4
  0.7 6.7 %shard_map.131 = bf16[64,32,128]{2,1,0:T(8,128)(2,1)} custom-call(bf16[3,1024,128]{2,1,0:T(8,128)(2,1)} %modes_hbm.1, s32[4,1536]{1,0:T(4,128)} %index_hbm.1, f32[4,1536]{1,0:T(4,128)} %interp_hbm.1, f32[3,1536]{1,0:T(4,128)} %normals_hbm.1), custom_call_target="tpu_custom_call" | custom-call | flops 1207959552 | bytes 1048576 | tf_op jit(solution)/shard_map/pallas_call | solution.py:109
  7.4 15.4 %all-to-all-start = ((bf16[128,16,128]{2,1,0:T(8,128)(2,1)}), bf16[128,16,128]{2,1,0:T(8,128)(2,1)S(1)}, u32[]{:S(2)}, u32[]{:S(2)}) async-start(bf16[128,16,128]{2,1,0:T(8,128)(2,1)} %bitcast.21), calls=%async_computation | async-start | bytes 1048576 | tf_op jit(solution)/shard_map/all_to_all | solution.py:532
  23.5 0.1 pad_add_fusion.place_ref
  23.6 0.0 copy-start.6
  23.6 0.5 copy-done.6
  24.1 0.0 copy-done.5
  24.1 0.0 copy-done.4
  24.1 1.6 %copy-done = bf16[1024,1024]{1,0:T(8,128)(2,1)S(1)} copy-done((bf16[1024,1024]{1,0:T(8,128)(2,1)S(1)}, bf16[1024,1024]{1,0:T(8,128)(2,1)}, u32[]{:S(2)}) %copy-start) | copy-done | bytes 2097176
  25.7 0.8 copy-done.8
  26.5 0.8 copy-done.9
  27.3 0.7 copy-done.10
  28.0 0.7 copy-done.11
  28.7 1.9 %shard_map.132 = (bf16[1024,128]{1,0:T(8,128)(2,1)S(1)}, bf16[64,128]{1,0:T(8,128)(2,1)S(1)}, f32[1,2048]{1,0:T(1,128)S(1)}, bf16[1024,256]{1,0:T(8,128)(2,1)S(1)}, f32[1024,128]{1,0:T(8,128)S(1)}) custom-call(s32[4]{0:T(128)S(1)} %pad_add_fusion.place_ref, s32[1]{0:T(128)S(6)} %copy.14.rank_ref, s32[1,128]{1,0:T(1,128)S(1)} %bitcast.20, ...), custom_call_target="tpu_custom_call" | custom-call | flops 4294967296 | bytes 8388608 | tf_op jit(solution)/shard_map/pallas_call | solution.py:176
  30.6 0.0 copy-start.2
  30.6 0.8 copy-done.2
  31.4 0.6 copy-done.12
  32.0 9.2 %all-to-all-done = bf16[128,16,128]{2,1,0:T(8,128)(2,1)S(1)} async-done(((bf16[128,16,128]{2,1,0:T(8,128)(2,1)}), bf16[128,16,128]{2,1,0:T(8,128)(2,1)S(1)}, u32[]{:S(2)}, u32[]{:S(2)}) %all-to-all-start) | async-done | bytes 524320 | tf_op jit(solution)/shard_map/all_to_all | solution.py:532
  41.2 0.7 copy-done.13
  41.9 0.9 %shard_map.133 = (bf16[1024,128]{1,0:T(8,128)(2,1)S(1)}, bf16[128,1024]{1,0:T(8,128)(2,1)S(1)}) custom-call(bf16[2048,128]{1,0:T(8,128)(2,1)S(1)} %bitcast.12, f32[1,2048]{1,0:T(1,128)S(1)} %copy-done.13), custom_call_target="tpu_custom_call" | custom-call | flops 536870912 | bytes 2097152 | tf_op jit(solution)/shard_map/pallas_call | solution.py:218
  42.8 0.1 collective-permute-start
  42.9 0.0 copy-done.1
  42.9 0.9 %shard_map.134 = (f32[1024,128]{1,0:T(8,128)S(1)}, bf16[64,128]{1,0:T(8,128)(2,1)S(1)}) custom-call(bf16[1024,128]{1,0:T(8,128)(2,1)S(1)} %get-tuple-element.14.normal_ref, bf16[1024,1024]{1,0:T(8,128)(2,1)S(1)} %copy-done.1, bf16[32,1024]{1,0:T(8,128)(2,1)S(1)} %bitcast.14, bf16[32,1024]{1,0:T(8,128)(2,1)S(1)} %bitcast.16), custom_call_target="tpu_custom_call" | custom-call | flops 536870912 | bytes 4194304 | tf_op jit(solution)/shard_map/pallas_call | solution.py:245
  43.8 0.6 collective-permute-done.other_ref
  44.4 0.0 copy-done.3
  44.4 0.0 copy-done.7
  44.4 1.0 %shard_map.135 = bf16[8,160,128]{2,1,0:T(8,128)(2,1)S(1)} custom-call(s32[4]{0:T(128)S(1)} %copy-done.7, f32[1024,128]{1,0:T(8,128)S(1)} %get-tuple-element.15.solved_ref, bf16[1024,256]{1,0:T(8,128)(2,1)S(1)} %get-tuple-element.16.scaled_ref, f32[1024,128]{1,0:T(8,128)S(1)} %copy-done.3, bf16[128,1024]{1,0:T(8,128)(2,1)S(1)} %get-tuple-element.18.turned_ref, ...), custom_call_target="tpu_custom_call" | custom-call | flops 268435456 | bytes 2097152 | tf_op jit(solution)/shard_map/pallas_call | solution.py:290
  45.4 16.7 %all_to_all.15.got_ref = bf16[8,160,128]{2,1,0:T(8,128)(2,1)S(1)} all-to-all(bf16[8,160,128]{2,1,0:T(8,128)(2,1)S(1)} %shard_map.135), channel_id=1, replica_groups=mesh['side'=2,'y'=4,'x'=4,'z'=8] {'z'}, dimensions={0} | all-to-all | bytes 655360 | tf_op jit(solution)/shard_map/all_to_all | solution.py:544
  62.2 2.4 %shard_map.136 = (f32[64,256]{1,0:T(8,128)S(1)}, bf16[16,144,128]{2,1,0:T(8,128)(2,1)S(1)}) custom-call(s32[4]{0:T(128)S(1)} %copy-done.7, bf16[8,160,128]{2,1,0:T(8,128)(2,1)S(1)} %all_to_all.15.got_ref), custom_call_target="tpu_custom_call" | custom-call | tf_op jit(solution)/shard_map/pallas_call | solution.py:409
  64.5 16.0 %all_to_all.16.got_ref = bf16[16,144,128]{2,1,0:T(8,128)(2,1)S(1)} all-to-all(bf16[16,144,128]{2,1,0:T(8,128)(2,1)S(1)} %get-tuple-element.21), channel_id=1, replica_groups=mesh['side'=2,'y'=4,'x'=4,'z'=8] {'y','x'}, dimensions={0} | all-to-all | bytes 1179648 | tf_op jit(solution)/shard_map/all_to_all | solution.py:546
  80.5 4.0 %shard_map.137 = (bf16[1024,128]{1,0:T(8,128)(2,1)}, f32[2,128]{1,0:T(2,128)}) custom-call(s32[4]{0:T(128)S(1)} %copy-done.7, bf16[16,144,128]{2,1,0:T(8,128)(2,1)S(1)} %all_to_all.16.got_ref, f32[64,256]{1,0:T(8,128)S(1)} %get-tuple-element.22.own_ref, f32[1024,128]{1,0:T(8,128)S(1)} %get-tuple-element.15.solved_ref, ...), custom_call_target="tpu_custom_call" | custom-call | tf_op jit(solution)/shard_map/pallas_call | solution.py:511
  (10 shorter events, 0.0 us)
Async XLA Ops:
  0.6 23.4 %copy-start.5 = (bf16[1024,32]{0,1:T(8,128)(2,1)S(1)}, bf16[1024,32]{0,1:T(8,128)(2,1)}, u32[]{:S(2)}) copy-start(bf16[1024,32]{0,1:T(8,128)(2,1)} %param.21) | copy-start | bytes 196612
  0.6 23.4 %copy-start.4 = (bf16[1024,32]{0,1:T(8,128)(2,1)S(1)}, bf16[1024,32]{0,1:T(8,128)(2,1)}, u32[]{:S(2)}) copy-start(bf16[1024,32]{0,1:T(8,128)(2,1)} %param.19) | copy-start | bytes 196612
  7.4 33.8 %all-to-all-start = ((bf16[128,16,128]{2,1,0:T(8,128)(2,1)}), bf16[128,16,128]{2,1,0:T(8,128)(2,1)S(1)}, u32[]{:S(2)}, u32[]{:S(2)}) async-start(bf16[128,16,128]{2,1,0:T(8,128)(2,1)} %bitcast.21), calls=%async_computation | async-start | bytes 1048576 | tf_op jit(solution)/shard_map/all_to_all | solution.py:532
  23.6 0.5 copy-start.6
  24.1 1.6 %copy-start = (bf16[1024,1024]{1,0:T(8,128)(2,1)S(1)}, bf16[1024,1024]{1,0:T(8,128)(2,1)}, u32[]{:S(2)}) copy-start(bf16[1024,1024]{1,0:T(8,128)(2,1)} %diag_ref.3) | copy-start | bytes 6291460
  25.7 0.8 copy-start.8
  26.5 0.8 copy-start.9
  27.3 0.7 copy-start.10
  28.0 0.7 copy-start.11
  28.7 14.2 %copy-start.1 = (bf16[1024,1024]{1,0:T(8,128)(2,1)S(1)}, bf16[1024,1024]{1,0:T(8,128)(2,1)}, u32[]{:S(2)}) copy-start(bf16[1024,1024]{1,0:T(8,128)(2,1)} %diag_ref.3) | copy-start | bytes 6291460
  30.6 0.8 copy-start.2
  31.4 0.6 copy-start.12
  41.2 0.7 copy-start.13
  41.9 2.6 %copy-start.3 = (f32[1024,128]{1,0:T(8,128)S(1)}, f32[1024,128]{1,0:T(8,128)}, u32[]{:S(2)}) copy-start(f32[1024,128]{1,0:T(8,128)} %copy-done.2) | copy-start | bytes 1572868
  41.9 2.6 %copy-start.7 = (s32[4]{0:T(128)S(1)}, s32[4]{0:T(128)}, u32[]{:S(2)}) copy-start(s32[4]{0:T(128)} %copy-done.6) | copy-start | bytes 52
  42.8 1.6 %collective-permute-start = (bf16[128,1024]{1,0:T(8,128)(2,1)S(1)}, bf16[128,1024]{1,0:T(8,128)(2,1)S(1)}, u32[]{:S(2)}, u32[]{:S(2)}) collective-permute-start(bf16[128,1024]{1,0:T(8,128)(2,1)S(1)} %get-tuple-element.18.turned_ref), channel_id=1, source_target_pairs={{0,128},{128,0},{1,129},{129,1},{2,130},{130,2},{3,131},{131,3},{4... | collective-permute-start | bytes 786440 | tf_op jit(solution)/shard_map/ppermute | solution.py:541

commit v5 on v4

--- a/solution.py
+++ b/solution.py
@@ -14,7 +14,7 @@
 VMEM = pl.BlockSpec(memory_space=pltpu.VMEM)
 SMEM = pl.BlockSpec(memory_space=pltpu.SMEM)
 HBM = pl.BlockSpec(memory_space=pltpu.HBM)
-STEPS, TURN, GROUPS = 4, 128, 2
+STEPS, TURN, GROUPS = 4, 128, 4
 TILE, LANES, ROWS = 32, 256, 192
 
 
@@ -317,10 +317,7 @@
     if mask is not None:
         factor = factor * mask
     high, low = halves(factor)
-    middle_high, middle_low = halves(middle)
-    rows = factor.shape[0]
-    first = mm(jnp.concatenate([high, low], axis=0), middle_high)
-    return total + (first[:rows] + first[rows:] + mm(high, middle_low))
+    return total + mm(jnp.concatenate([high, low, high], axis=1), tall(middle))
 
 
 def unit(offset):

time: 85.5 us -> 85.3 us (level)
  no operation moved by 1% of the time
where the time goes in v5:
time: 85.3 us; the launch traced here: 84.4 us
  blocking collectives  32.7 us (38%)
  Pallas kernels  17.7 us (21%)
  starting transfers between devices  15.5 us (18%)
  waiting for transfers between devices  9.75 us (11%)
  local copies, waits for them, and re-layouts  7.22 us (8%)
  between operations  1.39 us (2%)
    all_to_all x1, blocking collectives, body(): got = lax.all_to_all(send, 'z', split_axis=0, concat_axis=0, tiled=True)  16.7 us
    all_to_all x1, blocking collectives, body(): lax.all_to_all(send, ('y', 'x'), split_axis=0, concat_axis=0, tiled=True)  16 us
    all_to_all x1, starting transfers between devices, body(): lax.all_to_all(outgoing.reshape(devices, SLOT_ROWS, width), AXES, split_a...  15.4 us
    all_to_all x1, waiting for transfers between devices, body(): lax.all_to_all(outgoing.reshape(devices, SLOT_ROWS, width), AXES, split_a...  9.17 us
    unnamed x28, local copies, waits for them, and re-layouts  7.22 us
    pallas_call x1, Pallas kernels, interpolate(): pl.pallas_call(interp_kernel, in_specs=[HBM] * 4, out_specs=HBM, out_shap...  6.71 us
    pallas_call x1, Pallas kernels, outer(): pl.pallas_call(outer_kernel, in_specs=[SMEM] + [VMEM] * 4, out_specs=[VME...  3.75 us
    pallas_call x1, Pallas kernels, inner(): pl.pallas_call(inner_kernel, in_specs=[SMEM, VMEM], out_specs=[VMEM] * 2,...  2.46 us
  transfers between devices with their start and end apart: 2, of which 2 were waited for; matrix products, arithmetic and copies ran while one was open for 0% of the time, Pallas kernels for 3%

profile of v5, /device:TPU:2, one launch (start us, length us, event | category | flops | bytes accessed | tf_op | source)
XLA Modules:
  0.0 84.4 jit_solution(17847537128691380184)
XLA Ops:
  0.6 0.0 copy-start.5
  0.6 0.0 copy-start.4
  0.7 6.7 %shard_map.131 = bf16[64,32,128]{2,1,0:T(8,128)(2,1)} custom-call(bf16[3,1024,128]{2,1,0:T(8,128)(2,1)} %modes_hbm.1, s32[4,1536]{1,0:T(4,128)} %index_hbm.1, f32[4,1536]{1,0:T(4,128)} %interp_hbm.1, f32[3,1536]{1,0:T(4,128)} %normals_hbm.1), custom_call_target="tpu_custom_call" | custom-call | flops 1207959552 | bytes 1048576 | tf_op jit(solution)/shard_map/pallas_call | solution.py:109
  7.4 15.4 %all-to-all-start = ((bf16[128,16,128]{2,1,0:T(8,128)(2,1)}), bf16[128,16,128]{2,1,0:T(8,128)(2,1)S(1)}, u32[]{:S(2)}, u32[]{:S(2)}) async-start(bf16[128,16,128]{2,1,0:T(8,128)(2,1)} %bitcast.21), calls=%async_computation | async-start | bytes 1048576 | tf_op jit(solution)/shard_map/all_to_all | solution.py:529
  23.5 0.1 pad_add_fusion.place_ref
  23.6 0.5 copy-done.6
  24.1 0.0 copy-done.5
  24.1 0.0 copy-done.4
  24.1 0.0 copy-start
  24.1 1.6 %copy-done = bf16[1024,1024]{1,0:T(8,128)(2,1)S(1)} copy-done((bf16[1024,1024]{1,0:T(8,128)(2,1)S(1)}, bf16[1024,1024]{1,0:T(8,128)(2,1)}, u32[]{:S(2)}) %copy-start) | copy-done | bytes 2097176
  25.7 0.8 copy-done.8
  26.5 0.8 copy-done.9
  27.3 0.7 copy-done.10
  28.0 0.7 copy-done.11
  28.7 1.9 %shard_map.132 = (bf16[1024,128]{1,0:T(8,128)(2,1)S(1)}, bf16[64,128]{1,0:T(8,128)(2,1)S(1)}, f32[1,2048]{1,0:T(1,128)S(1)}, bf16[1024,256]{1,0:T(8,128)(2,1)S(1)}, f32[1024,128]{1,0:T(8,128)S(1)}) custom-call(s32[4]{0:T(128)S(1)} %pad_add_fusion.place_ref, s32[1]{0:T(128)S(6)} %copy.14.rank_ref, s32[1,128]{1,0:T(1,128)S(1)} %bitcast.20, ...), custom_call_target="tpu_custom_call" | custom-call | flops 4294967296 | bytes 8388608 | tf_op jit(solution)/shard_map/pallas_call | solution.py:176
  30.6 0.0 copy-start.2
  30.6 0.8 copy-done.2
  31.4 0.6 copy-done.12
  32.0 9.2 %all-to-all-done = bf16[128,16,128]{2,1,0:T(8,128)(2,1)S(1)} async-done(((bf16[128,16,128]{2,1,0:T(8,128)(2,1)}), bf16[128,16,128]{2,1,0:T(8,128)(2,1)S(1)}, u32[]{:S(2)}, u32[]{:S(2)}) %all-to-all-start) | async-done | bytes 524320 | tf_op jit(solution)/shard_map/all_to_all | solution.py:529
  41.2 0.7 copy-done.13
  41.9 0.9 %shard_map.133 = (bf16[1024,128]{1,0:T(8,128)(2,1)S(1)}, bf16[128,1024]{1,0:T(8,128)(2,1)S(1)}) custom-call(bf16[2048,128]{1,0:T(8,128)(2,1)S(1)} %bitcast.12, f32[1,2048]{1,0:T(1,128)S(1)} %copy-done.13), custom_call_target="tpu_custom_call" | custom-call | flops 536870912 | bytes 2097152 | tf_op jit(solution)/shard_map/pallas_call | solution.py:218
  42.8 0.1 collective-permute-start
  42.9 0.0 copy-done.1
  42.9 0.9 %shard_map.134 = (f32[1024,128]{1,0:T(8,128)S(1)}, bf16[64,128]{1,0:T(8,128)(2,1)S(1)}) custom-call(bf16[1024,128]{1,0:T(8,128)(2,1)S(1)} %get-tuple-element.14.normal_ref, bf16[1024,1024]{1,0:T(8,128)(2,1)S(1)} %copy-done.1, bf16[32,1024]{1,0:T(8,128)(2,1)S(1)} %bitcast.14, bf16[32,1024]{1,0:T(8,128)(2,1)S(1)} %bitcast.16), custom_call_target="tpu_custom_call" | custom-call | flops 536870912 | bytes 4194304 | tf_op jit(solution)/shard_map/pallas_call | solution.py:245
  43.8 0.6 collective-permute-done.other_ref
  44.4 0.0 copy-done.3
  44.4 0.0 copy-done.7
  44.4 1.0 %shard_map.135 = bf16[8,160,128]{2,1,0:T(8,128)(2,1)S(1)} custom-call(s32[4]{0:T(128)S(1)} %copy-done.7, f32[1024,128]{1,0:T(8,128)S(1)} %get-tuple-element.15.solved_ref, bf16[1024,256]{1,0:T(8,128)(2,1)S(1)} %get-tuple-element.16.scaled_ref, f32[1024,128]{1,0:T(8,128)S(1)} %copy-done.3, bf16[128,1024]{1,0:T(8,128)(2,1)S(1)} %get-tuple-element.18.turned_ref, ...), custom_call_target="tpu_custom_call" | custom-call | flops 268435456 | bytes 2097152 | tf_op jit(solution)/shard_map/pallas_call | solution.py:290
  45.4 16.7 %all_to_all.15.got_ref = bf16[8,160,128]{2,1,0:T(8,128)(2,1)S(1)} all-to-all(bf16[8,160,128]{2,1,0:T(8,128)(2,1)S(1)} %shard_map.135), channel_id=1, replica_groups=mesh['side'=2,'y'=4,'x'=4,'z'=8] {'z'}, dimensions={0} | all-to-all | bytes 655360 | tf_op jit(solution)/shard_map/all_to_all | solution.py:541
  62.2 2.5 %shard_map.136 = (f32[64,256]{1,0:T(8,128)S(1)}, bf16[16,144,128]{2,1,0:T(8,128)(2,1)S(1)}) custom-call(s32[4]{0:T(128)S(1)} %copy-done.7, bf16[8,160,128]{2,1,0:T(8,128)(2,1)S(1)} %all_to_all.15.got_ref), custom_call_target="tpu_custom_call" | custom-call | tf_op jit(solution)/shard_map/pallas_call | solution.py:406
  64.6 16.0 %all_to_all.16.got_ref = bf16[16,144,128]{2,1,0:T(8,128)(2,1)S(1)} all-to-all(bf16[16,144,128]{2,1,0:T(8,128)(2,1)S(1)} %get-tuple-element.21), channel_id=1, replica_groups=mesh['side'=2,'y'=4,'x'=4,'z'=8] {'y','x'}, dimensions={0} | all-to-all | bytes 1179648 | tf_op jit(solution)/shard_map/all_to_all | solution.py:543
  80.6 3.8 %shard_map.137 = (bf16[1024,128]{1,0:T(8,128)(2,1)}, f32[2,128]{1,0:T(2,128)}) custom-call(s32[4]{0:T(128)S(1)} %copy-done.7, bf16[16,144,128]{2,1,0:T(8,128)(2,1)S(1)} %all_to_all.16.got_ref, f32[64,256]{1,0:T(8,128)S(1)} %get-tuple-element.22.own_ref, f32[1024,128]{1,0:T(8,128)S(1)} %get-tuple-element.15.solved_ref, ...), custom_call_target="tpu_custom_call" | custom-call | tf_op jit(solution)/shard_map/pallas_call | solution.py:508
  (10 shorter events, 0.0 us)
Async XLA Ops:
  0.6 23.4 %copy-start.5 = (bf16[1024,32]{0,1:T(8,128)(2,1)S(1)}, bf16[1024,32]{0,1:T(8,128)(2,1)}, u32[]{:S(2)}) copy-start(bf16[1024,32]{0,1:T(8,128)(2,1)} %param.21) | copy-start | bytes 196612
  0.6 23.4 %copy-start.4 = (bf16[1024,32]{0,1:T(8,128)(2,1)S(1)}, bf16[1024,32]{0,1:T(8,128)(2,1)}, u32[]{:S(2)}) copy-start(bf16[1024,32]{0,1:T(8,128)(2,1)} %param.19) | copy-start | bytes 196612
  7.4 33.8 %all-to-all-start = ((bf16[128,16,128]{2,1,0:T(8,128)(2,1)}), bf16[128,16,128]{2,1,0:T(8,128)(2,1)S(1)}, u32[]{:S(2)}, u32[]{:S(2)}) async-start(bf16[128,16,128]{2,1,0:T(8,128)(2,1)} %bitcast.21), calls=%async_computation | async-start | bytes 1048576 | tf_op jit(solution)/shard_map/all_to_all | solution.py:529
  23.6 0.5 copy-start.6
  24.1 1.6 %copy-start = (bf16[1024,1024]{1,0:T(8,128)(2,1)S(1)}, bf16[1024,1024]{1,0:T(8,128)(2,1)}, u32[]{:S(2)}) copy-start(bf16[1024,1024]{1,0:T(8,128)(2,1)} %diag_ref.3) | copy-start | bytes 6291460
  25.7 0.8 copy-start.8
  26.5 0.8 copy-start.9
  27.3 0.7 copy-start.10
  28.0 0.7 copy-start.11
  28.7 14.2 %copy-start.1 = (bf16[1024,1024]{1,0:T(8,128)(2,1)S(1)}, bf16[1024,1024]{1,0:T(8,128)(2,1)}, u32[]{:S(2)}) copy-start(bf16[1024,1024]{1,0:T(8,128)(2,1)} %diag_ref.3) | copy-start | bytes 6291460
  30.6 0.8 copy-start.2
  31.4 0.6 copy-start.12
  41.2 0.7 copy-start.13
  41.9 2.6 %copy-start.3 = (f32[1024,128]{1,0:T(8,128)S(1)}, f32[1024,128]{1,0:T(8,128)}, u32[]{:S(2)}) copy-start(f32[1024,128]{1,0:T(8,128)} %copy-done.2) | copy-start | bytes 1572868
  41.9 2.6 %copy-start.7 = (s32[4]{0:T(128)S(1)}, s32[4]{0:T(128)}, u32[]{:S(2)}) copy-start(s32[4]{0:T(128)} %copy-done.6) | copy-start | bytes 52
  42.8 1.6 %collective-permute-start = (bf16[128,1024]{1,0:T(8,128)(2,1)S(1)}, bf16[128,1024]{1,0:T(8,128)(2,1)S(1)}, u32[]{:S(2)}, u32[]{:S(2)}) collective-permute-start(bf16[128,1024]{1,0:T(8,128)(2,1)S(1)} %get-tuple-element.18.turned_ref), channel_id=1, source_target_pairs={{0,128},{128,0},{1,129},{129,1},{2,130},{130,2},{3,131},{131,3},{4... | collective-permute-start | bytes 786440 | tf_op jit(solution)/shard_map/ppermute | solution.py:538

commit v6 on v5

--- a/solution.py
+++ b/solution.py
@@ -317,7 +317,12 @@
     if mask is not None:
         factor = factor * mask
     high, low = halves(factor)
-    return total + mm(jnp.concatenate([high, low, high], axis=1), tall(middle))
+    rows, wide = factor.shape[0], middle.shape[1]
+    if rows != 3 * RANK:
+        return total + mm(jnp.concatenate([high, low, high], axis=1), tall(middle))
+    both = jnp.concatenate(halves(middle), axis=1)
+    first = mm(jnp.concatenate([high, low], axis=0), both)
+    return total + (first[:rows, :wide] + first[rows:, :wide] + first[:rows, wide:])
 
 
 def unit(offset):

time: 85.3 us -> 85.2 us (level)
  no operation moved by 1% of the time
where the time goes in v6:
time: 85.2 us; the launch traced here: 84.3 us
  blocking collectives  32.7 us (38%)
  Pallas kernels  17.6 us (21%)
  starting transfers between devices  15.5 us (18%)
  waiting for transfers between devices  9.75 us (11%)
  local copies, waits for them, and re-layouts  7.22 us (8%)
  between operations  1.4 us (2%)
    all_to_all x1, blocking collectives, body(): got = lax.all_to_all(send, 'z', split_axis=0, concat_axis=0, tiled=True)  16.7 us
    all_to_all x1, blocking collectives, body(): lax.all_to_all(send, ('y', 'x'), split_axis=0, concat_axis=0, tiled=True)  16 us
    all_to_all x1, starting transfers between devices, body(): lax.all_to_all(outgoing.reshape(devices, SLOT_ROWS, width), AXES, split_a...  15.4 us
    all_to_all x1, waiting for transfers between devices, body(): lax.all_to_all(outgoing.reshape(devices, SLOT_ROWS, width), AXES, split_a...  9.17 us
    unnamed x28, local copies, waits for them, and re-layouts  7.22 us
    pallas_call x1, Pallas kernels, interpolate(): pl.pallas_call(interp_kernel, in_specs=[HBM] * 4, out_specs=HBM, out_shap...  6.71 us
    pallas_call x1, Pallas kernels, outer(): pl.pallas_call(outer_kernel, in_specs=[SMEM] + [VMEM] * 4, out_specs=[VME...  3.76 us
    pallas_call x1, Pallas kernels, inner(): pl.pallas_call(inner_kernel, in_specs=[SMEM, VMEM], out_specs=[VMEM] * 2,...  2.35 us
  transfers between devices with their start and end apart: 2, of which 2 were waited for; matrix products, arithmetic and copies ran while one was open for 0% of the time, Pallas kernels for 3%

profile of v6, /device:TPU:2, one launch (start us, length us, event | category | flops | bytes accessed | tf_op | source)
XLA Modules:
  0.0 84.3 jit_solution(8667226581787067971)
XLA Ops:
  0.6 0.0 copy-start.5
  0.6 0.0 copy-start.4
  0.7 6.7 %shard_map.131 = bf16[64,32,128]{2,1,0:T(8,128)(2,1)} custom-call(bf16[3,1024,128]{2,1,0:T(8,128)(2,1)} %modes_hbm.1, s32[4,1536]{1,0:T(4,128)} %index_hbm.1, f32[4,1536]{1,0:T(4,128)} %interp_hbm.1, f32[3,1536]{1,0:T(4,128)} %normals_hbm.1), custom_call_target="tpu_custom_call" | custom-call | flops 1207959552 | bytes 1048576 | tf_op jit(solution)/shard_map/pallas_call | solution.py:109
  7.4 15.4 %all-to-all-start = ((bf16[128,16,128]{2,1,0:T(8,128)(2,1)}), bf16[128,16,128]{2,1,0:T(8,128)(2,1)S(1)}, u32[]{:S(2)}, u32[]{:S(2)}) async-start(bf16[128,16,128]{2,1,0:T(8,128)(2,1)} %bitcast.21), calls=%async_computation | async-start | bytes 1048576 | tf_op jit(solution)/shard_map/all_to_all | solution.py:534
  23.5 0.1 pad_add_fusion.place_ref
  23.6 0.5 copy-done.6
  24.1 0.0 copy-done.5
  24.1 0.0 copy-done.4
  24.1 0.0 copy-start
  24.1 1.6 %copy-done = bf16[1024,1024]{1,0:T(8,128)(2,1)S(1)} copy-done((bf16[1024,1024]{1,0:T(8,128)(2,1)S(1)}, bf16[1024,1024]{1,0:T(8,128)(2,1)}, u32[]{:S(2)}) %copy-start) | copy-done | bytes 2097176
  25.7 0.8 copy-done.8
  26.5 0.8 copy-done.9
  27.3 0.7 copy-done.10
  28.0 0.7 copy-done.11
  28.7 1.9 %shard_map.132 = (bf16[1024,128]{1,0:T(8,128)(2,1)S(1)}, bf16[64,128]{1,0:T(8,128)(2,1)S(1)}, f32[1,2048]{1,0:T(1,128)S(1)}, bf16[1024,256]{1,0:T(8,128)(2,1)S(1)}, f32[1024,128]{1,0:T(8,128)S(1)}) custom-call(s32[4]{0:T(128)S(1)} %pad_add_fusion.place_ref, s32[1]{0:T(128)S(6)} %copy.14.rank_ref, s32[1,128]{1,0:T(1,128)S(1)} %bitcast.20, ...), custom_call_target="tpu_custom_call" | custom-call | flops 4294967296 | bytes 8388608 | tf_op jit(solution)/shard_map/pallas_call | solution.py:176
  30.6 0.0 copy-start.2
  30.6 0.8 copy-done.2
  31.4 0.6 copy-done.12
  32.0 9.2 %all-to-all-done = bf16[128,16,128]{2,1,0:T(8,128)(2,1)S(1)} async-done(((bf16[128,16,128]{2,1,0:T(8,128)(2,1)}), bf16[128,16,128]{2,1,0:T(8,128)(2,1)S(1)}, u32[]{:S(2)}, u32[]{:S(2)}) %all-to-all-start) | async-done | bytes 524320 | tf_op jit(solution)/shard_map/all_to_all | solution.py:534
  41.2 0.7 copy-done.13
  41.9 0.9 %shard_map.133 = (bf16[1024,128]{1,0:T(8,128)(2,1)S(1)}, bf16[128,1024]{1,0:T(8,128)(2,1)S(1)}) custom-call(bf16[2048,128]{1,0:T(8,128)(2,1)S(1)} %bitcast.12, f32[1,2048]{1,0:T(1,128)S(1)} %copy-done.13), custom_call_target="tpu_custom_call" | custom-call | flops 536870912 | bytes 2097152 | tf_op jit(solution)/shard_map/pallas_call | solution.py:218
  42.8 0.1 collective-permute-start
  42.9 0.0 copy-done.1
  42.9 0.9 %shard_map.134 = (f32[1024,128]{1,0:T(8,128)S(1)}, bf16[64,128]{1,0:T(8,128)(2,1)S(1)}) custom-call(bf16[1024,128]{1,0:T(8,128)(2,1)S(1)} %get-tuple-element.14.normal_ref, bf16[1024,1024]{1,0:T(8,128)(2,1)S(1)} %copy-done.1, bf16[32,1024]{1,0:T(8,128)(2,1)S(1)} %bitcast.14, bf16[32,1024]{1,0:T(8,128)(2,1)S(1)} %bitcast.16), custom_call_target="tpu_custom_call" | custom-call | flops 536870912 | bytes 4194304 | tf_op jit(solution)/shard_map/pallas_call | solution.py:245
  43.8 0.6 collective-permute-done.other_ref
  44.4 0.0 copy-done.3
  44.4 0.0 copy-done.7
  44.4 1.0 %shard_map.135 = bf16[8,160,128]{2,1,0:T(8,128)(2,1)S(1)} custom-call(s32[4]{0:T(128)S(1)} %copy-done.7, f32[1024,128]{1,0:T(8,128)S(1)} %get-tuple-element.15.solved_ref, bf16[1024,256]{1,0:T(8,128)(2,1)S(1)} %get-tuple-element.16.scaled_ref, f32[1024,128]{1,0:T(8,128)S(1)} %copy-done.3, bf16[128,1024]{1,0:T(8,128)(2,1)S(1)} %get-tuple-element.18.turned_ref, ...), custom_call_target="tpu_custom_call" | custom-call | flops 268435456 | bytes 2097152 | tf_op jit(solution)/shard_map/pallas_call | solution.py:290
  45.4 16.7 %all_to_all.15.got_ref = bf16[8,160,128]{2,1,0:T(8,128)(2,1)S(1)} all-to-all(bf16[8,160,128]{2,1,0:T(8,128)(2,1)S(1)} %shard_map.135), channel_id=1, replica_groups=mesh['side'=2,'y'=4,'x'=4,'z'=8] {'z'}, dimensions={0} | all-to-all | bytes 655360 | tf_op jit(solution)/shard_map/all_to_all | solution.py:546
  62.2 2.4 %shard_map.136 = (f32[64,256]{1,0:T(8,128)S(1)}, bf16[16,144,128]{2,1,0:T(8,128)(2,1)S(1)}) custom-call(s32[4]{0:T(128)S(1)} %copy-done.7, bf16[8,160,128]{2,1,0:T(8,128)(2,1)S(1)} %all_to_all.15.got_ref), custom_call_target="tpu_custom_call" | custom-call | tf_op jit(solution)/shard_map/pallas_call | solution.py:411
  64.5 16.0 %all_to_all.16.got_ref = bf16[16,144,128]{2,1,0:T(8,128)(2,1)S(1)} all-to-all(bf16[16,144,128]{2,1,0:T(8,128)(2,1)S(1)} %get-tuple-element.21), channel_id=1, replica_groups=mesh['side'=2,'y'=4,'x'=4,'z'=8] {'y','x'}, dimensions={0} | all-to-all | bytes 1179648 | tf_op jit(solution)/shard_map/all_to_all | solution.py:548
  80.5 3.8 %shard_map.137 = (bf16[1024,128]{1,0:T(8,128)(2,1)}, f32[2,128]{1,0:T(2,128)}) custom-call(s32[4]{0:T(128)S(1)} %copy-done.7, bf16[16,144,128]{2,1,0:T(8,128)(2,1)S(1)} %all_to_all.16.got_ref, f32[64,256]{1,0:T(8,128)S(1)} %get-tuple-element.22.own_ref, f32[1024,128]{1,0:T(8,128)S(1)} %get-tuple-element.15.solved_ref, ...), custom_call_target="tpu_custom_call" | custom-call | tf_op jit(solution)/shard_map/pallas_call | solution.py:513
  (10 shorter events, 0.0 us)
Async XLA Ops:
  0.6 23.4 %copy-start.5 = (bf16[1024,32]{0,1:T(8,128)(2,1)S(1)}, bf16[1024,32]{0,1:T(8,128)(2,1)}, u32[]{:S(2)}) copy-start(bf16[1024,32]{0,1:T(8,128)(2,1)} %param.21) | copy-start | bytes 196612
  0.6 23.4 %copy-start.4 = (bf16[1024,32]{0,1:T(8,128)(2,1)S(1)}, bf16[1024,32]{0,1:T(8,128)(2,1)}, u32[]{:S(2)}) copy-start(bf16[1024,32]{0,1:T(8,128)(2,1)} %param.19) | copy-start | bytes 196612
  7.4 33.8 %all-to-all-start = ((bf16[128,16,128]{2,1,0:T(8,128)(2,1)}), bf16[128,16,128]{2,1,0:T(8,128)(2,1)S(1)}, u32[]{:S(2)}, u32[]{:S(2)}) async-start(bf16[128,16,128]{2,1,0:T(8,128)(2,1)} %bitcast.21), calls=%async_computation | async-start | bytes 1048576 | tf_op jit(solution)/shard_map/all_to_all | solution.py:534
  23.6 0.5 copy-start.6
  24.1 1.6 %copy-start = (bf16[1024,1024]{1,0:T(8,128)(2,1)S(1)}, bf16[1024,1024]{1,0:T(8,128)(2,1)}, u32[]{:S(2)}) copy-start(bf16[1024,1024]{1,0:T(8,128)(2,1)} %diag_ref.3) | copy-start | bytes 6291460
  25.7 0.8 copy-start.8
  26.5 0.8 copy-start.9
  27.3 0.7 copy-start.10
  28.0 0.7 copy-start.11
  28.7 14.2 %copy-start.1 = (bf16[1024,1024]{1,0:T(8,128)(2,1)S(1)}, bf16[1024,1024]{1,0:T(8,128)(2,1)}, u32[]{:S(2)}) copy-start(bf16[1024,1024]{1,0:T(8,128)(2,1)} %diag_ref.3) | copy-start | bytes 6291460
  30.6 0.8 copy-start.2
  31.4 0.6 copy-start.12
  41.2 0.7 copy-start.13
  41.9 2.6 %copy-start.3 = (f32[1024,128]{1,0:T(8,128)S(1)}, f32[1024,128]{1,0:T(8,128)}, u32[]{:S(2)}) copy-start(f32[1024,128]{1,0:T(8,128)} %copy-done.2) | copy-start | bytes 1572868
  41.9 2.6 %copy-start.7 = (s32[4]{0:T(128)S(1)}, s32[4]{0:T(128)}, u32[]{:S(2)}) copy-start(s32[4]{0:T(128)} %copy-done.6) | copy-start | bytes 52
  42.8 1.6 %collective-permute-start = (bf16[128,1024]{1,0:T(8,128)(2,1)S(1)}, bf16[128,1024]{1,0:T(8,128)(2,1)S(1)}, u32[]{:S(2)}, u32[]{:S(2)}) collective-permute-start(bf16[128,1024]{1,0:T(8,128)(2,1)S(1)} %get-tuple-element.18.turned_ref), channel_id=1, source_target_pairs={{0,128},{128,0},{1,129},{129,1},{2,130},{130,2},{3,131},{131,3},{4... | collective-permute-start | bytes 786440 | tf_op jit(solution)/shard_map/ppermute | solution.py:543
